TPU v7x, 256 devices: a whole 4x4x8 slice. The times are simulated.
256 devices in a mesh: leaf: 32 (over z, x), sib: 8 (over y, core).
Axes of the slice: x: 4, y: 4, z: 8, core: 2. Of those that a mesh axis runs over, the one named last changes fastest.
Arguments:
- sources: float32 [131072, 128], P(('leaf', 'sib')), may hold values from -8 to 8
- ordering: int32 [131072], P(('leaf', 'sib')), may hold values from 0 to 131071, as said below
- diagonal_inverse: float32 [512, 256, 256], P(('leaf', 'sib')), as said below
- low_rank: float32 [131072, 128], P(('leaf', 'sib'))
- nearby_blocks: bfloat16 [512, 8, 256, 256], P(('leaf', 'sib')), may hold values from -0.125 to 0.125
- near_index: int32 [512, 8], P(('leaf', 'sib')), may hold values from 0 to 511, as said below
Outputs:
- solution: float32 [131072, 128], P(('leaf', 'sib'))
- coefficients: float32 [128, 128], replicated
Inputs may be any that keep to these rules, and one draw needn't show every extreme that they name: `ordering`: each catalog row appears once, and the rows of leaf block i are i * 256 to i * 256 + 255. `near_index`: each entry names a leaf block other than its row's own, at most 2 blocks away from it; the distance 2 occurs. `diagonal_inverse`: each block is symmetric positive definite.
All inputs are finite; a program needn't handle non-finite values.
Results may differ from a plain program's by a relative error of at most 0.0034.
Values may be sent and summed in bfloat16 or wider, within the bound.
No kernel may reach another device: no remote copies, remote signals or barrier semaphores. Data moves between devices by JAX's collectives and lax.ppermute only.
A program may use at most 64 MiB of HBM per device.

v0:
```python
import jax
import jax.numpy as jnp
from jax import lax
from jax.sharding import Mesh
from jax.sharding import PartitionSpec as P

ITERS = 4
LEAF_SIB = ("leaf_0", "leaf_1", "sib_0", "sib_1")
SIB = ("sib_0", "sib_1")
LEAF = ("leaf_0", "leaf_1")


def with_halo(array, sides, width):
    edges = {}
    for axis, dim in sides:
        size, length = (lax.axis_size(axis), array.shape[dim])
        up = [(i, (i + 1) % size) for i in range(size - 1)]
        last = lax.slice_in_dim(array, length - width, length, axis=dim)
        first = lax.slice_in_dim(array, 0, width, axis=dim)
        edges[dim] = (
            lax.ppermute(last, axis, up),
            lax.ppermute(first, axis, [(b, a) for a, b in up]),
        )
    done = []
    for _, dim in sides:
        low, high = edges[dim]
        around = [(width, width) if d in done else (0, 0) for d in range(array.ndim)]
        array = jnp.concatenate([jnp.pad(low, around), array, jnp.pad(high, around)], axis=dim)
        done.append(dim)
    return array


def from_everyone(array, axis):
    size = lax.axis_size(axis)
    return lax.all_to_all(
        jnp.broadcast_to(array[None], (size, *array.shape)), axis, 0, 0, tiled=True
    )


def of_everyone(array, axis):
    everything = from_everyone(array, axis)
    return jnp.sum(everything, axis=0)


def padded_to(lines, size):
    spare = -len(lines) % size
    return jnp.pad(lines, [(0, spare)] + [(0, 0)] * (lines.ndim - 1))


def joined_along(parts, dim):
    parts = jnp.moveaxis(parts, 0, dim)
    shape = parts.shape
    return parts.reshape(*shape[:dim], shape[dim] * shape[dim + 1], *shape[dim + 2 :])


def collect(array, axis, dim):
    parts = from_everyone(array, axis)
    return joined_along(parts, dim)


def split_up(array, dim, size):
    before, after = (array.shape[:dim], array.shape[dim + 1 :])
    return jnp.moveaxis(array.reshape(*before, size, -1, *after), dim, 0)


def summed_on_arrival(array, axis, dim):
    parts = split_up(array, dim, lax.axis_size(axis))
    arrived = lax.all_to_all(parts, axis, split_axis=0, concat_axis=0, tiled=True)
    return arrived.sum(axis=0)


def total_of(array, axes):
    lines = array.reshape(-1, array.shape[-1])
    padded = padded_to(lines, lax.axis_size(axes))
    whole = collect(summed_on_arrival(padded, axes, 0), axes, 0)
    return lax.slice_in_dim(whole, 0, len(lines)).reshape(array.shape)


def whole_of(array, axes, dim):
    far, near = axes
    parts = from_everyone(from_everyone(array, far), near)
    return joined_along(parts.swapaxes(0, 1).reshape(-1, *array.shape), dim)


def sum_in_two_steps(array, axes, dim):
    far, near = axes
    parts = split_up(array, dim, lax.axis_size(far))
    nearer = summed_on_arrival(parts, near, dim + 1)
    arrived = lax.all_to_all(nearer, far, split_axis=0, concat_axis=0, tiled=True)
    return arrived.sum(axis=0)


def sum_by_parts(array, axes):
    padded = padded_to(array, lax.axis_size(axes[0]) * lax.axis_size(axes[1]))
    whole = whole_of(sum_in_two_steps(padded, axes, 0), axes, 0)
    return lax.slice_in_dim(whole, 0, len(array)).reshape(array.shape)


def in_one(arrays, axis):
    ends = [0]
    for a in arrays:
        ends.append(ends[-1] + a.size)
    total = sum_by_parts(jnp.concatenate([a.ravel() for a in arrays]), axis)
    return tuple((total[b:e].reshape(a.shape) for a, b, e in zip(arrays, ends, ends[1:])))


def neighbours(rounded, leaf_dev):
    return with_halo(rounded, ((LEAF_SIB, 0),), leaf_dev)


def totals(projection_partial):
    partner_sum = of_everyone(projection_partial, SIB)
    return total_of(partner_sum, LEAF)


def on_device(sources, ordering, diagonal_inverse, low_rank, nearby_blocks, near_index):
    highest_setting = lax.Precision.HIGHEST
    leaf_dev = diagonal_inverse.shape[0]
    leaf_size = diagonal_inverse.shape[1]
    columns = sources.shape[1]
    rank_width = low_rank.shape[1]
    position = lax.axis_index(LEAF) * lax.axis_size(SIB) + lax.axis_index(SIB)
    first_row = position * (leaf_dev * leaf_size)
    local_rows = ordering - first_row
    ordered_rows = sources[local_rows].reshape(leaf_dev, leaf_size, columns)
    block_list = low_rank.reshape(leaf_dev, leaf_size, rank_width)
    lifted_vector = jnp.einsum(
        "zym,zmw->zyw", diagonal_inverse, block_list, precision=highest_setting
    )
    core_partial = jnp.einsum("wju,wjp->up", block_list, lifted_vector, precision=highest_setting)
    scaled_rows = jnp.einsum(
        "zym,zmw->zyw", diagonal_inverse, ordered_rows, precision=highest_setting
    )
    projection_partial = jnp.einsum(
        "wju,wjp->up", block_list, scaled_rows, precision=highest_setting
    )
    core_sum, projected_rows = in_one(
        (core_partial, projection_partial), (("leaf_0", "leaf_1"), ("sib_0", "sib_1"))
    )
    triangle = jnp.linalg.cholesky(jnp.eye(rank_width, dtype=jnp.float32) + core_sum)

    def finish(current_scaled, projected_now):
        coefficients = jax.scipy.linalg.cho_solve((triangle, True), projected_now)
        result_vector = current_scaled - jnp.einsum(
            "eqb,bd->eqd", lifted_vector, coefficients, precision=highest_setting
        )
        return (result_vector, coefficients)

    iterate, coefficients = finish(scaled_rows, projected_rows)
    first_block = (position - 1) * leaf_dev
    targets = near_index - first_block
    for sweep in range(ITERS):
        rounded = iterate.astype(jnp.bfloat16)
        window = neighbours(rounded, leaf_dev)
        piece_list = window[targets]
        image_vector = jnp.einsum(
            "ptog,ptgh->poh", nearby_blocks, piece_list, preferred_element_type=jnp.float32
        )
        scaled_rows = jnp.einsum(
            "zym,zmw->zyw", diagonal_inverse, ordered_rows - image_vector, precision=highest_setting
        )
        projection_partial = jnp.einsum(
            "wju,wjp->up", block_list, scaled_rows, precision=highest_setting
        )
        projected_rows = totals(projection_partial)
        iterate, coefficients = finish(scaled_rows, projected_rows)
    return (iterate.reshape(leaf_dev * leaf_size, columns), coefficients)


def solution(mesh):
    torus = Mesh(mesh.devices.reshape(8, 4, 4, 2), ("leaf_0", "leaf_1", "sib_0", "sib_1"))
    placed = (
        P(LEAF_SIB, None),
        P(LEAF_SIB),
        P(LEAF_SIB, None, None),
        P(LEAF_SIB, None),
        P(LEAF_SIB, None, None, None),
        P(LEAF_SIB, None),
    )
    return jax.shard_map(
        on_device, mesh=torus, in_specs=placed, out_specs=(P(LEAF_SIB, None), P()), check_vma=False
    )
```

profile of v0, /device:TPU:1, one launch (start us, length us, event | category | flops | bytes accessed | tf_op | source)
XLA Modules:
  0.0 353.5 jit_solution(5623588213110201519)
XLA Ops:
  8.9 11.5 %all_to_all.85 = f32[8,32,128]{2,1,0:T(8,128)} all-to-all(f32[8,32,128]{2,1,0:T(8,128)S(1)} %maximum_bitcast_fusion), channel_id=1, replica_groups=mesh['leaf_0'=8,'leaf_1'=4,'sib_0'=4,'sib_1'=2] {'sib_0','sib_1'}, dimensions={0} | all-to-all | bytes 262144 | tf_op jit(solution)/shard_map/all_to_all | solution.py:68
  21.3 19.1 %all_to_all.86 = f32[32,1,128]{2,1,0:T(1,128)S(1)} all-to-all(f32[32,1,128]{2,1,0:T(1,128)S(1)} %bitcast.218), channel_id=1, replica_groups=mesh['leaf_0'=8,'leaf_1'=4,'sib_0'=4,'sib_1'=2] {'leaf_0','leaf_1'}, dimensions={0} | all-to-all | bytes 32768 | tf_op jit(solution)/shard_map/all_to_all | solution.py:89
  40.4 11.6 %all_to_all.87 = f32[32,1,128]{2,1,0:T(1,128)S(1)} all-to-all(f32[32,1,128]{2,1,0:T(1,128)S(1)} %broadcast_in_dim.29), channel_id=1, replica_groups=mesh['leaf_0'=8,'leaf_1'=4,'sib_0'=4,'sib_1'=2] {'leaf_0','leaf_1'}, dimensions={0} | all-to-all | bytes 32768 | tf_op jit(solution)/shard_map/all_to_all | solution.py:35
  52.7 7.3 %all-to-all-start.3 = ((f32[8,32,128]{2,1,0:T(8,128)}), f32[8,32,128]{2,1,0:T(8,128)}, u32[]{:S(2)}, u32[]{:S(2)}) async-start(f32[8,32,128]{2,1,0:T(8,128)} %broadcast_in_dim.31), calls=%async_computation.3 | async-start | bytes 262144 | tf_op jit(solution)/shard_map/all_to_all | solution.py:35
  60.0 5.4 %all-to-all-done.3 = f32[8,32,128]{2,1,0:T(8,128)} async-done(((f32[8,32,128]{2,1,0:T(8,128)}), f32[8,32,128]{2,1,0:T(8,128)}, u32[]{:S(2)}, u32[]{:S(2)}) %all-to-all-start.3) | async-done | bytes 131104 | tf_op jit(solution)/shard_map/all_to_all | solution.py:35
  68.0 11.7 %cholesky.20 = f32[128,128]{1,0:T(8,128)S(1)} custom-call(f32[128,128]{1,0:T(8,128)S(1)} %fusion.27), custom_call_target="Cholesky" | custom-call | tf_op jit(solution)/shard_map/jit(cholesky)/cholesky | solution.py:140
  81.0 9.8 %custom-call.12 = f32[1,128,128]{1,2,0:T(8,128)S(1)} custom-call(f32[1,128,128]{2,1,0:T(8,128)S(1)} %fusion.8), custom_call_target="InvertDiagBlocksLowerTriangular" | custom-call | tf_op jit(solution)/shard_map/jit(_cho_solve)/triangular_solve | solution.py:143
  93.2 2.8 collective-permute-start.1
  96.0 3.0 collective-permute-start
  102.9 2.6 gather_fusion.1
  105.5 2.0 fusion
  110.8 14.0 %all_to_all.88 = f32[8,128,128]{2,1,0:T(8,128)} all-to-all(f32[8,128,128]{2,1,0:T(8,128)S(1)} %broadcast_in_dim.33), channel_id=1, replica_groups=mesh['leaf_0'=8,'leaf_1'=4,'sib_0'=4,'sib_1'=2] {'sib_0','sib_1'}, dimensions={0} | all-to-all | bytes 1048576 | tf_op jit(solution)/shard_map/all_to_all | solution.py:35
  126.5 19.5 %all_to_all.89 = f32[32,4,128]{2,1,0:T(4,128)S(1)} all-to-all(f32[32,4,128]{2,1,0:T(4,128)} %bitcast.214), channel_id=1, replica_groups=mesh['leaf_0'=8,'leaf_1'=4,'sib_0'=4,'sib_1'=2] {'leaf_0','leaf_1'}, dimensions={0} | all-to-all | bytes 131072 | tf_op jit(solution)/shard_map/all_to_all | solution.py:68
  146.0 11.9 %all_to_all.90 = f32[32,4,128]{2,1,0:T(4,128)S(1)} all-to-all(f32[32,4,128]{2,1,0:T(4,128)S(1)} %broadcast_in_dim.34), channel_id=1, replica_groups=mesh['leaf_0'=8,'leaf_1'=4,'sib_0'=4,'sib_1'=2] {'leaf_0','leaf_1'}, dimensions={0} | all-to-all | bytes 131072 | tf_op jit(solution)/shard_map/all_to_all | solution.py:35
  159.8 5.5 %collective-permute-start.3 = (bf16[2,256,128]{1,2,0:T(8,128)(2,1)S(1)}, bf16[2,256,128]{1,2,0:T(8,128)(2,1)S(1)}, u32[]{:S(2)}, u32[]{:S(2)}) collective-permute-start(bf16[2,256,128]{1,2,0:T(8,128)(2,1)S(1)} %fusion.5), channel_id=1, source_target_pairs={{1,0},{2,1},{3,2},{4,3},{5,4},{6,5},{7,6},{8,7},{9,8},{10,9},{11,1... | collective-permute-start | bytes 393224 | tf_op jit(solution)/shard_map/ppermute | solution.py:22
  165.4 2.1 collective-permute-start.2
  170.2 2.6 gather_fusion.2
  178.2 13.9 %all_to_all.91 = f32[8,128,128]{2,1,0:T(8,128)} all-to-all(f32[8,128,128]{2,1,0:T(8,128)S(1)} %broadcast_in_dim.35), channel_id=1, replica_groups=mesh['leaf_0'=8,'leaf_1'=4,'sib_0'=4,'sib_1'=2] {'sib_0','sib_1'}, dimensions={0} | all-to-all | bytes 1048576 | tf_op jit(solution)/shard_map/all_to_all | solution.py:35
  193.8 17.8 %all_to_all.92 = f32[32,4,128]{2,1,0:T(4,128)S(1)} all-to-all(f32[32,4,128]{2,1,0:T(4,128)} %bitcast.215), channel_id=1, replica_groups=mesh['leaf_0'=8,'leaf_1'=4,'sib_0'=4,'sib_1'=2] {'leaf_0','leaf_1'}, dimensions={0} | all-to-all | bytes 131072 | tf_op jit(solution)/shard_map/all_to_all | solution.py:68
  211.6 11.9 %all_to_all.93 = f32[32,4,128]{2,1,0:T(4,128)S(1)} all-to-all(f32[32,4,128]{2,1,0:T(4,128)S(1)} %broadcast_in_dim.36), channel_id=1, replica_groups=mesh['leaf_0'=8,'leaf_1'=4,'sib_0'=4,'sib_1'=2] {'leaf_0','leaf_1'}, dimensions={0} | all-to-all | bytes 131072 | tf_op jit(solution)/shard_map/all_to_all | solution.py:35
  225.4 5.5 %collective-permute-start.5 = (bf16[2,256,128]{1,2,0:T(8,128)(2,1)S(1)}, bf16[2,256,128]{1,2,0:T(8,128)(2,1)S(1)}, u32[]{:S(2)}, u32[]{:S(2)}) collective-permute-start(bf16[2,256,128]{1,2,0:T(8,128)(2,1)S(1)} %fusion.6), channel_id=1, source_target_pairs={{1,0},{2,1},{3,2},{4,3},{5,4},{6,5},{7,6},{8,7},{9,8},{10,9},{11,1... | collective-permute-start | bytes 393224 | tf_op jit(solution)/shard_map/ppermute | solution.py:22
  231.0 2.1 collective-permute-start.4
  235.8 2.6 gather_fusion.3
  243.8 13.9 %all_to_all.94 = f32[8,128,128]{2,1,0:T(8,128)} all-to-all(f32[8,128,128]{2,1,0:T(8,128)S(1)} %broadcast_in_dim.37), channel_id=1, replica_groups=mesh['leaf_0'=8,'leaf_1'=4,'sib_0'=4,'sib_1'=2] {'sib_0','sib_1'}, dimensions={0} | all-to-all | bytes 1048576 | tf_op jit(solution)/shard_map/all_to_all | solution.py:35
  259.4 17.8 %all_to_all.95 = f32[32,4,128]{2,1,0:T(4,128)S(1)} all-to-all(f32[32,4,128]{2,1,0:T(4,128)} %bitcast.216), channel_id=1, replica_groups=mesh['leaf_0'=8,'leaf_1'=4,'sib_0'=4,'sib_1'=2] {'leaf_0','leaf_1'}, dimensions={0} | all-to-all | bytes 131072 | tf_op jit(solution)/shard_map/all_to_all | solution.py:68
  277.2 11.9 %all_to_all.96 = f32[32,4,128]{2,1,0:T(4,128)S(1)} all-to-all(f32[32,4,128]{2,1,0:T(4,128)S(1)} %broadcast_in_dim.38), channel_id=1, replica_groups=mesh['leaf_0'=8,'leaf_1'=4,'sib_0'=4,'sib_1'=2] {'leaf_0','leaf_1'}, dimensions={0} | all-to-all | bytes 131072 | tf_op jit(solution)/shard_map/all_to_all | solution.py:35
  291.0 5.5 %collective-permute-start.7 = (bf16[2,256,128]{1,2,0:T(8,128)(2,1)S(1)}, bf16[2,256,128]{1,2,0:T(8,128)(2,1)S(1)}, u32[]{:S(2)}, u32[]{:S(2)}) collective-permute-start(bf16[2,256,128]{1,2,0:T(8,128)(2,1)S(1)} %fusion.7), channel_id=1, source_target_pairs={{1,0},{2,1},{3,2},{4,3},{5,4},{6,5},{7,6},{8,7},{9,8},{10,9},{11,1... | collective-permute-start | bytes 393224 | tf_op jit(solution)/shard_map/ppermute | solution.py:22
  296.5 2.1 collective-permute-start.6
  301.3 2.6 gather_fusion.4
  307.2 13.9 %all_to_all.97 = f32[8,128,128]{2,1,0:T(8,128)} all-to-all(f32[8,128,128]{2,1,0:T(8,128)S(1)} %broadcast_in_dim.39), channel_id=1, replica_groups=mesh['leaf_0'=8,'leaf_1'=4,'sib_0'=4,'sib_1'=2] {'sib_0','sib_1'}, dimensions={0} | all-to-all | bytes 1048576 | tf_op jit(solution)/shard_map/all_to_all | solution.py:35
  322.2 17.6 %all_to_all.98 = f32[32,4,128]{2,1,0:T(4,128)S(1)} all-to-all(f32[32,4,128]{2,1,0:T(4,128)S(1)} %bitcast.217), channel_id=1, replica_groups=mesh['leaf_0'=8,'leaf_1'=4,'sib_0'=4,'sib_1'=2] {'leaf_0','leaf_1'}, dimensions={0} | all-to-all | bytes 131072 | tf_op jit(solution)/shard_map/all_to_all | solution.py:68
  339.8 11.9 %all_to_all.99 = f32[32,4,128]{2,1,0:T(4,128)S(1)} all-to-all(f32[32,4,128]{2,1,0:T(4,128)S(1)} %broadcast_in_dim.40), channel_id=1, replica_groups=mesh['leaf_0'=8,'leaf_1'=4,'sib_0'=4,'sib_1'=2] {'leaf_0','leaf_1'}, dimensions={0} | all-to-all | bytes 131072 | tf_op jit(solution)/shard_map/all_to_all | solution.py:35
  (104 shorter events, 59.0 us)
Async XLA Ops:
  0.6 104.8 %copy-start = (bf16[2,8,256,256]{3,2,1,0:T(8,128)(2,1)S(1)}, bf16[2,8,256,256]{3,2,1,0:T(8,128)(2,1)}, u32[]{:S(2)}) copy-start(bf16[2,8,256,256]{3,2,1,0:T(8,128)(2,1)} %param.12) | copy-start | bytes 6291460
  0.6 5.9 %copy-start.1 = (f32[2,256,256]{2,1,0:T(8,128)S(1)}, f32[2,256,256]{2,1,0:T(8,128)}, u32[]{:S(2)}) copy-start(f32[2,256,256]{2,1,0:T(8,128)} %param.10) | copy-start | bytes 1572868
  0.7 4.2 %copy-start.2 = (f32[512,128]{1,0:T(8,128)S(1)}, f32[512,128]{1,0:T(8,128)}, u32[]{:S(2)}) copy-start(f32[512,128]{1,0:T(8,128)} %param.8) | copy-start | bytes 786436
  3.3 5.0 %copy-start.3 = (f32[512,128]{1,0:T(8,128)S(1)}, f32[512,128]{1,0:T(8,128)}, u32[]{:S(2)}) copy-start(f32[512,128]{1,0:T(8,128)} %param.11) | copy-start | bytes 786436
  8.2 90.7 %copy-start.9 = (s32[2,8]{1,0:T(2,128)S(1)}, s32[2,8]{1,0:T(2,128)}, u32[]{:S(2)}) copy-start(s32[2,8]{1,0:T(2,128)} %param.13) | copy-start | bytes 196
  52.7 12.7 %all-to-all-start.3 = ((f32[8,32,128]{2,1,0:T(8,128)}), f32[8,32,128]{2,1,0:T(8,128)}, u32[]{:S(2)}, u32[]{:S(2)}) async-start(f32[8,32,128]{2,1,0:T(8,128)} %broadcast_in_dim.31), calls=%async_computation.3 | async-start | bytes 262144 | tf_op jit(solution)/shard_map/all_to_all | solution.py:35
  66.3 0.6 copy-start.7
  93.2 7.0 %collective-permute-start.1 = (bf16[2,256,128]{1,2,0:T(8,128)(2,1)}, bf16[2,256,128]{1,2,0:T(8,128)(2,1)}, u32[]{:S(2)}, u32[]{:S(2)}) collective-permute-start(bf16[2,256,128]{1,2,0:T(8,128)(2,1)} %fusion.4), channel_id=1, source_target_pairs={{1,0},{2,1},{3,2},{4,3},{5,4},{6,5},{7,6},{8,7},{9,8},{10,9},{11,1... | collective-permute-start | bytes 393224 | tf_op jit(solution)/shard_map/ppermute | solution.py:22
  96.0 5.0 %collective-permute-start = (bf16[2,256,128]{1,2,0:T(8,128)(2,1)}, bf16[2,256,128]{1,2,0:T(8,128)(2,1)}, u32[]{:S(2)}, u32[]{:S(2)}) collective-permute-start(bf16[2,256,128]{1,2,0:T(8,128)(2,1)} %fusion.4), channel_id=1, source_target_pairs={{0,1},{1,2},{2,3},{3,4},{4,5},{5,6},{6,7},{7,8},{8,9},{9,10},{10,1... | collective-permute-start | bytes 393224 | tf_op jit(solution)/shard_map/ppermute | solution.py:21
  108.1 0.7 copy-start.4
  159.8 8.4 %collective-permute-start.3 = (bf16[2,256,128]{1,2,0:T(8,128)(2,1)S(1)}, bf16[2,256,128]{1,2,0:T(8,128)(2,1)S(1)}, u32[]{:S(2)}, u32[]{:S(2)}) collective-permute-start(bf16[2,256,128]{1,2,0:T(8,128)(2,1)S(1)} %fusion.5), channel_id=1, source_target_pairs={{1,0},{2,1},{3,2},{4,3},{5,4},{6,5},{7,6},{8,7},{9,8},{10,9},{11,1... | collective-permute-start | bytes 393224 | tf_op jit(solution)/shard_map/ppermute | solution.py:22
  165.4 4.0 %collective-permute-start.2 = (bf16[2,256,128]{1,2,0:T(8,128)(2,1)S(1)}, bf16[2,256,128]{1,2,0:T(8,128)(2,1)S(1)}, u32[]{:S(2)}, u32[]{:S(2)}) collective-permute-start(bf16[2,256,128]{1,2,0:T(8,128)(2,1)S(1)} %fusion.5), channel_id=1, source_target_pairs={{0,1},{1,2},{2,3},{3,4},{4,5},{5,6},{6,7},{7,8},{8,9},{9,10},{10,1... | collective-permute-start | bytes 393224 | tf_op jit(solution)/shard_map/ppermute | solution.py:21
  175.5 0.7 copy-start.5
  225.4 8.4 %collective-permute-start.5 = (bf16[2,256,128]{1,2,0:T(8,128)(2,1)S(1)}, bf16[2,256,128]{1,2,0:T(8,128)(2,1)S(1)}, u32[]{:S(2)}, u32[]{:S(2)}) collective-permute-start(bf16[2,256,128]{1,2,0:T(8,128)(2,1)S(1)} %fusion.6), channel_id=1, source_target_pairs={{1,0},{2,1},{3,2},{4,3},{5,4},{6,5},{7,6},{8,7},{9,8},{10,9},{11,1... | collective-permute-start | bytes 393224 | tf_op jit(solution)/shard_map/ppermute | solution.py:22
  231.0 4.0 %collective-permute-start.4 = (bf16[2,256,128]{1,2,0:T(8,128)(2,1)S(1)}, bf16[2,256,128]{1,2,0:T(8,128)(2,1)S(1)}, u32[]{:S(2)}, u32[]{:S(2)}) collective-permute-start(bf16[2,256,128]{1,2,0:T(8,128)(2,1)S(1)} %fusion.6), channel_id=1, source_target_pairs={{0,1},{1,2},{2,3},{3,4},{4,5},{5,6},{6,7},{7,8},{8,9},{9,10},{10,1... | collective-permute-start | bytes 393224 | tf_op jit(solution)/shard_map/ppermute | solution.py:21
  241.0 0.7 copy-start.6
  291.0 8.4 %collective-permute-start.7 = (bf16[2,256,128]{1,2,0:T(8,128)(2,1)S(1)}, bf16[2,256,128]{1,2,0:T(8,128)(2,1)S(1)}, u32[]{:S(2)}, u32[]{:S(2)}) collective-permute-start(bf16[2,256,128]{1,2,0:T(8,128)(2,1)S(1)} %fusion.7), channel_id=1, source_target_pairs={{1,0},{2,1},{3,2},{4,3},{5,4},{6,5},{7,6},{8,7},{9,8},{10,9},{11,1... | collective-permute-start | bytes 393224 | tf_op jit(solution)/shard_map/ppermute | solution.py:22
  296.5 4.0 %collective-permute-start.6 = (bf16[2,256,128]{1,2,0:T(8,128)(2,1)S(1)}, bf16[2,256,128]{1,2,0:T(8,128)(2,1)S(1)}, u32[]{:S(2)}, u32[]{:S(2)}) collective-permute-start(bf16[2,256,128]{1,2,0:T(8,128)(2,1)S(1)} %fusion.7), channel_id=1, source_target_pairs={{0,1},{1,2},{2,3},{3,4},{4,5},{5,6},{6,7},{7,8},{8,9},{9,10},{10,1... | collective-permute-start | bytes 393224 | tf_op jit(solution)/shard_map/ppermute | solution.py:21
  352.2 1.3 copy-start.8
where the time goes:
time: 357 us; the launch traced here: 353 us
  blocking collectives  218 us (61%)
  other arithmetic  36.1 us (10%)
  starting transfers between devices  35.9 us (10%)
  matrix products  28.5 us (8%)
  local copies, waits for them, and re-layouts  21.6 us (6%)
  waiting for transfers between devices  12 us (3%)
    all_to_all x9, blocking collectives, from_everyone(): lax.all_to_all(jnp.broadcast_to(array[None], (size, *array.shape)), axis,...  115 us
    all_to_all x5, blocking collectives, summed_on_arrival(): lax.all_to_all(parts, axis, split_axis=0, concat_axis=0, tiled=True)  84 us
    ppermute x4, starting transfers between devices, with_halo(): lax.ppermute(first, axis, [(b, a) for a, b in up])  19.4 us
    all_to_all x1, blocking collectives, sum_in_two_steps(): lax.all_to_all(nearer, far, split_axis=0, concat_axis=0, tiled=True)  19.1 us
    another operation x3, other arithmetic, on_device(): jnp.linalg.cholesky(jnp.eye(rank_width, dtype=jnp.float32) + core_sum)  12.4 us
    another operation x2, other arithmetic, finish(): coefficients = jax.scipy.linalg.cho_solve((triangle, True), projected_now)  10.5 us
    gather x4, local copies, waits for them, and re-layouts, on_device(): piece_list = window[targets]  10.4 us
    ppermute x4, starting transfers between devices, with_halo(): lax.ppermute(last, axis, up)  9.26 us
  transfers between devices with their start and end apart: 9, of which 8 were waited for; matrix products, arithmetic and copies ran while one was open for 0% of the time, Pallas kernels for 0%

commit v1 on v0

v1 whole, which is shorter than its diff:
```python
import jax
import jax.numpy as jnp
from jax import lax
from jax.experimental import pallas as pl
from jax.experimental.pallas import tpu as pltpu
from jax.sharding import Mesh
from jax.sharding import PartitionSpec as P

ITERS = 4
LEVELS = ITERS + 1
AXES = ("leaf_0", "leaf_1", "sib_0", "sib_1")
PLANE = ("leaf_1", "sib_0", "sib_1")
LINE = "leaf_0"
F32 = jnp.float32
BF16 = jnp.bfloat16
VMEM_LIMIT = 16 * 1024 * 1024
VMEM = pl.BlockSpec(memory_space=pltpu.VMEM)
ANY = pl.BlockSpec(memory_space=pl.ANY)
HBM = pl.BlockSpec(memory_space=pltpu.HBM)
SMEM = pl.BlockSpec(memory_space=pltpu.SMEM)
TILE = 8
LANES = 128


def params():
    return pltpu.CompilerParams(vmem_limit_bytes=VMEM_LIMIT)


def dot(a, b):
    return jnp.dot(a, b, preferred_element_type=F32)


def dot_rows(a, b):
    return lax.dot_general(a, b, (((0,), (0,)), ((), ())), preferred_element_type=F32)


def exact_dot(a, b):
    return jnp.dot(a, b, preferred_element_type=F32, precision=lax.Precision.HIGHEST)


def parts(value):
    high = value.astype(BF16)
    return high, (value - high.astype(F32)).astype(BF16)


def dot3(a, b):
    (a_high, a_low), (b_high, b_low) = a, b
    return dot(a_high, b_high) + (dot(a_high, b_low) + dot(a_low, b_high))


def shape(dims, dtype=F32):
    return jax.ShapeDtypeStruct(dims, dtype)


def first_kernel(
    order_hbm, source_hbm, inverse_hbm, factor_hbm, near_hbm,
    basis_ref, sent_ref, high_ref, low_ref, near_ref, order_ref, source, factor, inverse, sems,
):
    leaves, size, _ = inverse.shape
    columns = source.shape[1]
    pairs = (
        (order_hbm, order_ref),
        (source_hbm, source),
        (factor_hbm, factor),
        (inverse_hbm, inverse),
        (near_hbm, near_ref),
    )
    copies = [pltpu.make_async_copy(a, b, sems.at[i]) for i, (a, b) in enumerate(pairs)]
    for copy in copies:
        copy.start()
    row = lax.broadcasted_iota(jnp.int32, (size, size), 0)
    copies[0].wait()
    copies[1].wait()
    ordered = []
    for leaf in range(leaves):
        here = pl.ds(leaf * size, size)
        order = order_ref[:, leaf * size : (leaf + 1) * size] & (size - 1)
        chosen = (row == order).astype(F32).astype(BF16)
        ordered.append(dot_rows(chosen, jnp.concatenate(parts(source[here, :]), axis=1)).astype(BF16))
    copies[2].wait()
    copies[3].wait()
    for leaf in range(leaves):
        here = pl.ds(leaf * size, size)
        factor_high, factor_low = parts(factor[here, :])
        inverse_high, inverse_low = parts(inverse[leaf])
        high_ref[leaf] = inverse_high
        low_ref[leaf] = inverse_low
        high = jnp.concatenate([ordered[leaf][:, :columns], factor_high], axis=1)
        low = jnp.concatenate([ordered[leaf][:, columns:], factor_low], axis=1)
        basis = dot3((inverse_high, inverse_low), (high, low))
        basis_ref[here, :] = basis
        sent_ref[here, :] = basis.astype(BF16)
    copies[4].wait()


def first_step(order, sources, inverse, factor, near):
    rows, columns = sources.shape
    width = columns + factor.shape[1]
    return pl.pallas_call(
        first_kernel,
        out_shape=(
            shape((rows, width)),
            shape((rows, width), BF16),
            shape(inverse.shape, BF16),
            shape(inverse.shape, BF16),
            shape(near.shape, BF16),
        ),
        in_specs=[HBM] * 5,
        out_specs=(VMEM,) * 5,
        scratch_shapes=[
            pltpu.VMEM(order.shape, jnp.int32),
            pltpu.VMEM(sources.shape, F32),
            pltpu.VMEM(factor.shape, F32),
            pltpu.VMEM(inverse.shape, F32),
            pltpu.SemaphoreType.DMA((5,)),
        ],
        compiler_params=params(),
        name="first_step",
    )(*(pltpu.with_memory_space_constraint(v, pltpu.HBM) for v in (order, sources, inverse, factor, near)))


def turn_kernel(factor_ref, basis_ref, high_ref, low_ref, sum_ref):
    factor_high, factor_low = parts(factor_ref[...])
    high_ref[...] = factor_high.T
    low_ref[...] = factor_low.T
    sum_ref[...] = dot3((high_ref[...], low_ref[...]), parts(basis_ref[...]))


def turned(factor, basis):
    rows, rank = factor.shape
    return pl.pallas_call(
        turn_kernel,
        out_shape=(shape((rank, rows), BF16), shape((rank, rows), BF16), shape((rank, basis.shape[1]))),
        compiler_params=params(),
        name="turned",
    )(factor, basis)


def project_kernel(high_ref, low_ref, value_ref, sum_ref):
    sum_ref[...] = dot3((high_ref[...], low_ref[...]), parts(value_ref[...]))


def projected(high, low, value):
    return pl.pallas_call(
        project_kernel,
        out_shape=shape((high.shape[0], value.shape[1])),
        compiler_params=params(),
        name="projected",
    )(high, low, value)


def sweep_kernel(
    target_ref, own_ref, pair_ref, cross_ref, near_ref, high_ref, low_ref, basis_ref, _,
    next_ref, sent_ref, window,
):
    leaves, near, size, _ = near_ref.shape
    for place, ref in enumerate((pair_ref, own_ref, cross_ref)):
        for leaf in range(leaves):
            window[place * leaves + leaf] = ref[leaf * size : (leaf + 1) * size, :]
    for leaf in range(leaves):
        here = pl.ds(leaf * size, size)
        image = dot(near_ref[leaf, 0], window[target_ref[leaf, 0]])
        for k in range(1, near):
            image += dot(near_ref[leaf, k], window[target_ref[leaf, k]])
        value = basis_ref[here, :] - dot3((high_ref[leaf], low_ref[leaf]), parts(image))
        next_ref[here, :] = value
        sent_ref[here, :] = value.astype(BF16)


def sweep(targets, own, pair, cross, near, high, low, basis, sums):
    leaves, size = near.shape[0], near.shape[2]
    return pl.pallas_call(
        sweep_kernel,
        out_shape=(shape(basis.shape), shape(basis.shape, BF16)),
        in_specs=[SMEM] + [VMEM] * 7 + [ANY],
        out_specs=(VMEM, VMEM),
        scratch_shapes=[pltpu.VMEM((3 * leaves, size, basis.shape[1]), BF16)],
        compiler_params=params(),
        name="sweep",
    )(targets, own, pair, cross, near, high, low, basis, sums)


def place_of(chunk, rank):
    half, rest = divmod(chunk * TILE, rank)
    return slice(rest, rest + TILE), slice(half * LANES, half * LANES + LANES)


def pack_kernel(high_ref, low_ref, value_ref, *refs):
    sum_refs, (out_ref, changes) = refs[:ITERS], refs[ITERS:]
    rank = changes.shape[1]
    sums = [ref[...] for ref in sum_refs]
    sums.append(dot3((high_ref[...], low_ref[...]), parts(value_ref[...])))
    start = sums[0].astype(BF16).astype(F32)
    changes[0] = start
    changes[1] = sums[0] - start
    for j in range(1, LEVELS):
        changes[j + 1] = sums[j] - sums[j - 1]
    for chunk in range(out_ref.shape[0]):
        rows, lanes = place_of(chunk, rank)
        for j in range(0, LEVELS + 1, 2):
            both = jnp.concatenate([changes[j, rows, lanes], changes[j + 1, rows, lanes]], axis=0)
            out_ref[chunk, j * TILE : (j + 2) * TILE, :] = both.astype(BF16)


def packed(high, low, value, sums, count):
    rank, width = sums[0].shape
    return pl.pallas_call(
        pack_kernel,
        out_shape=shape((count, (LEVELS + 1) * TILE, LANES), BF16),
        scratch_shapes=[pltpu.VMEM((LEVELS + 1, rank, width), F32)],
        compiler_params=params(),
        name="packed",
    )(high, low, value, *sums)


def add_kernel(in_ref, out_ref):
    total = in_ref[0].astype(F32)
    for i in range(1, in_ref.shape[0]):
        total += in_ref[i].astype(F32)
    total = jnp.concatenate([total[:TILE] + total[TILE : 2 * TILE], total[2 * TILE :]], axis=0)
    for i in range(out_ref.shape[0]):
        out_ref[i] = total


def added(arrived, count):
    return pl.pallas_call(
        add_kernel,
        out_shape=shape((count, arrived.shape[1] - TILE, LANES)),
        compiler_params=params(),
        name="added",
    )(arrived)


def split_kernel(in_ref, out_ref):
    total = in_ref[0]
    for i in range(1, in_ref.shape[0]):
        total += in_ref[i]
    start = total[:TILE].astype(BF16).astype(F32)
    total = jnp.concatenate([start, total[:TILE] - start, total[TILE:]], axis=0).astype(BF16)
    for i in range(out_ref.shape[0]):
        out_ref[i] = total


def split(arrived, count):
    return pl.pallas_call(
        split_kernel,
        out_shape=shape((count, arrived.shape[1] + TILE, LANES), BF16),
        compiler_params=params(),
        name="split",
    )(arrived)


def inverse_of(core, eye):
    diagonal = 1.0 / jnp.sum(core * eye, axis=0, keepdims=True)
    size = jnp.max(jnp.sum(jnp.abs(core), axis=0))
    spread = jnp.max(jnp.sum(jnp.abs(eye - core * diagonal), axis=0))
    scale = jnp.where(spread < 0.9, diagonal, 2.0 / (1.0 + size))

    def keep_going(state):
        step, _, rest = state
        return jnp.logical_and(step < 48, jnp.max(jnp.abs(rest)) > 1e-6)

    def improve(state):
        step, value, rest = state
        value = value + exact_dot(value, rest)
        return step + 1, value, eye - exact_dot(core, value)

    return lax.while_loop(keep_going, improve, (0, eye * scale, eye - core * scale))[1]


def last_kernel(arrived_ref, *refs):
    basis_refs, (solution_ref, coefficients_ref, total) = refs[:LEVELS], refs[LEVELS:]
    rank = total.shape[1]
    columns = total.shape[2] - rank
    for chunk in range(arrived_ref.shape[0]):
        rows, lanes = place_of(chunk, rank)
        for j in range(0, LEVELS + 1, 2):
            both = arrived_ref[chunk, j * TILE : (j + 2) * TILE, :].astype(F32)
            if j == 0:
                total[0, rows, lanes] = both[:TILE] + both[TILE:]
            else:
                total[j - 1, rows, lanes] = both[:TILE]
                total[j, rows, lanes] = both[TILE:]
    eye = (
        lax.broadcasted_iota(jnp.int32, (rank, rank), 0) == lax.broadcasted_iota(jnp.int32, (rank, rank), 1)
    ).astype(F32)
    core_inverse = parts(inverse_of(eye + total[0, :, columns:], eye))
    change = [None] + [parts(dot3(core_inverse, parts(total[j, :, columns:]))) for j in range(1, LEVELS)]
    right = total[0, :, :columns]
    plain = [dot3(core_inverse, parts(right))]
    for k in range(1, LEVELS):
        right += total[k, :, :columns]
        plain.append(dot3(core_inverse, parts(right)))
    found, halves = [], []
    for k in range(LEVELS):
        value = plain[k]
        for j in range(k, 0, -1):
            value -= dot3(change[j], halves[k - j])
        found.append(value)
        halves.append(parts(value))
    coefficients_ref[...] = found[-1]
    solution = basis_refs[-1][:, :columns]
    for k in range(LEVELS):
        weight = found[ITERS - k]
        if k < ITERS:
            weight = weight - found[ITERS - k - 1]
        solution -= dot3(parts(basis_refs[k][:, columns:]), parts(weight))
    solution_ref[...] = solution


def last_step(arrived, bases, rank):
    rows, width = bases[0].shape
    return pl.pallas_call(
        last_kernel,
        out_shape=(shape((rows, width - rank)), shape((rank, width - rank))),
        scratch_shapes=[pltpu.VMEM((LEVELS, rank, width), F32)],
        compiler_params=params(),
        name="last_step",
    )(arrived, *bases)


def exchanged(array, axes):
    return lax.all_to_all(array, axes, 0, 0, tiled=True)


def on_device(sources, ordering, inverse, low_rank, nearby_blocks, near_index):
    leaves = inverse.shape[0]
    count = lax.axis_size(AXES)
    position = lax.axis_index(AXES)
    even = position % 2 == 0
    offset = near_index - position * leaves
    after = 2 * leaves
    targets = jnp.where(
        offset < 0,
        offset + leaves + jnp.where(even, after, 0),
        jnp.where(offset < leaves, offset + leaves, offset - leaves + jnp.where(even, 0, after)),
    )
    within = [(i, i ^ 1) for i in range(count)]
    across = [(i, j) for i in range(1, count - 1) for j in (i + 1 if i % 2 else i - 1,)]
    basis, sent, inverse_high, inverse_low, near = first_step(
        ordering.reshape(1, -1), sources, inverse, low_rank, nearby_blocks
    )
    bases, sums = [basis], []
    for k in range(ITERS):
        cross = lax.ppermute(sent, AXES, across)
        pair = lax.ppermute(sent, AXES, within)
        if k == 0:
            high, low, latest = turned(low_rank, basis)
        else:
            latest = projected(high, low, bases[-1])
        sums.append(latest)
        value, sent = sweep(targets, sent, pair, cross, near, inverse_high, inverse_low, basis, latest)
        bases.append(value)
    plane, line = lax.axis_size(PLANE), lax.axis_size(LINE)
    arrived = exchanged(packed(high, low, bases[-1], sums, plane), PLANE)
    arrived = exchanged(added(arrived, line), LINE)
    arrived = exchanged(split(arrived, plane), PLANE)
    return last_step(arrived, bases, low_rank.shape[1])


def solution(mesh):
    torus = Mesh(mesh.devices.reshape(8, 4, 4, 2), AXES)
    placed = (
        P(AXES, None),
        P(AXES),
        P(AXES, None, None),
        P(AXES, None),
        P(AXES, None, None, None),
        P(AXES, None),
    )
    return jax.shard_map(
        on_device, mesh=torus, in_specs=placed, out_specs=(P(AXES, None), P()), check_vma=False
    )
```

time: 357 us -> 124 us (0.35)
  blocking collectives: 218 us -> 68 us
  other arithmetic: 36.1 us -> 0.01 us
  matrix products: 28.5 us -> 0 us
  Pallas kernels: 0 us -> 24.5 us
  local copies, waits for them, and re-layouts: 21.6 us -> 0.01 us
  starting transfers between devices: 35.9 us -> 15.9 us
    all_to_all x15 -> x3, blocking collectives: 218 us -> 68 us  [exchanged(): return lax.all_to_all(array, axes, 0, 0, tiled=True)]
    dot_general x21 -> x0, matrix products: 25.2 us -> none  [the longest x4 8.09 us: on_device(): jnp.einsum('ptog,ptgh->poh', nearby_blocks, piece_list, preferred_element...]
    pallas_call x0 -> x13, Pallas kernels: none -> 24.5 us  [the longest x4 11.1 us: sweep(): pl.pallas_call(sweep_kernel, out_shape=(shape(basis.shape), shape(basis.s...]
    another operation x5 -> x0, other arithmetic: 22.9 us -> none  [the longest x3 12.4 us: on_device(): jnp.linalg.cholesky(jnp.eye(rank_width, dtype=jnp.float32) + core_sum)]
    ppermute x8, starting transfers between devices: 28.6 us -> 15.9 us  [the longest x4 15.5 us: on_device(): cross = lax.ppermute(sent, AXES, across)]
    gather x5 -> x0, local copies, waits for them, and re-layouts: 12 us -> none  [the longest x4 10.4 us: on_device(): piece_list = window[targets]]
    ppermute x8, waiting for transfers between devices: 6.64 us -> 14.8 us  [the longest x4 14.8 us: on_device(): cross = lax.ppermute(sent, AXES, across)]
    reduce_sum x10 -> x0, other arithmetic: 7.33 us -> none  [the longest x4 6.19 us: of_everyone(): return jnp.sum(everything, axis=0)]
  transfers between devices with their start and end apart: 9 -> 8, of which waited for: 8 -> 4; matrix products, arithmetic and copies ran while one was open for 0% -> 0% of each run, Pallas kernels for 0% -> 1%
where the time goes in v1:
time: 124 us
  blocking collectives  68 us (55%)
  Pallas kernels  24.5 us (20%)
  starting transfers between devices  15.9 us (13%)
  waiting for transfers between devices  14.8 us (12%)
    all_to_all x3, blocking collectives, exchanged(): return lax.all_to_all(array, axes, 0, 0, tiled=True)  68 us
    ppermute x4, starting transfers between devices, on_device(): cross = lax.ppermute(sent, AXES, across)  15.5 us
    ppermute x4, waiting for transfers between devices, on_device(): cross = lax.ppermute(sent, AXES, across)  14.8 us
    pallas_call x4, Pallas kernels, sweep(): pl.pallas_call(sweep_kernel, out_shape=(shape(basis.shape), shape(basis.s...  11.1 us
    pallas_call x1, Pallas kernels, last_step(): pl.pallas_call(last_kernel, out_shape=(shape((rows, width - rank)), shape...  9.07 us
    pallas_call x1, Pallas kernels, first_step(): pl.pallas_call(first_kernel, out_shape=(shape((rows, width)), shape((rows...  2.72 us
  transfers between devices with their start and end apart: 8, of which 4 were waited for; matrix products, arithmetic and copies ran while one was open for 0% of the time, Pallas kernels for 1%

profile of v1, /device:TPU:1, one launch (start us, length us, event | category | flops | bytes accessed | tf_op | source)
XLA Modules:
  0.0 124.0 jit_solution(18156342752683792707)
XLA Ops:
  0.6 0.0 copy-start
  0.7 2.7 %first_step.1 = (f32[512,256]{1,0:T(8,128)S(1)}, bf16[512,256]{1,0:T(8,128)(2,1)}, bf16[2,256,256]{2,1,0:T(8,128)(2,1)S(1)}, bf16[2,256,256]{2,1,0:T(8,128)(2,1)S(1)}, bf16[2,8,256,256]{3,2,1,0:T(8,128)(2,1)S(1)}) custom-call(s32[1,512]{1,0:T(1,128)} %bitcast.1, f32[512,128]{1,0:T(8,128)} %source_hbm.1, f32[2,256,256]{2,1,0:T(8,128)} %inverse_hbm.1, ...), custom_call_target="tpu_custom_call" | custom-call | tf_op jit(solution)/shard_map/first_step/pallas_call | solution.py:99
  3.4 4.6 %collective-permute-start.1 = (bf16[512,256]{1,0:T(8,128)(2,1)}, bf16[512,256]{1,0:T(8,128)(2,1)}, u32[]{:S(2)}, u32[]{:S(2)}) collective-permute-start(bf16[512,256]{1,0:T(8,128)(2,1)} %get-tuple-element.20.own_ref), channel_id=1, source_target_pairs={{1,2},{2,1},{3,4},{4,3},{5,6},{6,5},{7,8},{8,7},{9,10},{10,9},{11,... | collective-permute-start | bytes 786440 | tf_op jit(solution)/shard_map/ppermute | solution.py:345
  8.0 0.1 collective-permute-start
  8.1 0.3 turned.1
  8.4 3.9 %collective-permute-done.1.cross_ref = bf16[512,256]{1,0:T(8,128)(2,1)} collective-permute-done((bf16[512,256]{1,0:T(8,128)(2,1)}, bf16[512,256]{1,0:T(8,128)(2,1)}, u32[]{:S(2)}, u32[]{:S(2)}) %collective-permute-start.1) | collective-permute-done | bytes 262176 | tf_op jit(solution)/shard_map/ppermute | solution.py:345
  12.3 0.0 collective-permute-done.pair_ref
  12.3 3.0 %sweep.4 = (f32[512,256]{1,0:T(8,128)S(1)}, bf16[512,256]{1,0:T(8,128)(2,1)S(1)}) custom-call(s32[2,8]{1,0:T(2,128)S(1)} %compare_select_fusion.1.target_ref, bf16[512,256]{1,0:T(8,128)(2,1)} %get-tuple-element.20.own_ref, bf16[512,256]{1,0:T(8,128)(2,1)} %collective-permute-done.pair_ref, bf16[512,256]{1,0:T(8,128)(2,1)} %collective-permute-done.1.cross_ref, ...), custom_call_target="tpu_custom_call" | custom-call | tf_op jit(solution)/shard_map/sweep/pallas_call | solution.py:172
  15.4 3.6 %collective-permute-start.3 = (bf16[512,256]{1,0:T(8,128)(2,1)S(1)}, bf16[512,256]{1,0:T(8,128)(2,1)S(1)}, u32[]{:S(2)}, u32[]{:S(2)}) collective-permute-start(bf16[512,256]{1,0:T(8,128)(2,1)S(1)} %get-tuple-element.25.own_ref), channel_id=1, source_target_pairs={{1,2},{2,1},{3,4},{4,3},{5,6},{6,5},{7,8},{8,7},{9,10},{10,9},{11,... | collective-permute-start | bytes 786440 | tf_op jit(solution)/shard_map/ppermute | solution.py:345
  19.0 0.1 collective-permute-start.2
  19.1 0.3 projected.3._.refs_1_
  19.4 3.6 %collective-permute-done.3.cross_ref = bf16[512,256]{1,0:T(8,128)(2,1)S(1)} collective-permute-done((bf16[512,256]{1,0:T(8,128)(2,1)S(1)}, bf16[512,256]{1,0:T(8,128)(2,1)S(1)}, u32[]{:S(2)}, u32[]{:S(2)}) %collective-permute-start.3) | collective-permute-done | bytes 262176 | tf_op jit(solution)/shard_map/ppermute | solution.py:345
  23.1 0.0 collective-permute-done.2.pair_ref
  23.1 2.5 %sweep.5 = (f32[512,256]{1,0:T(8,128)S(1)}, bf16[512,256]{1,0:T(8,128)(2,1)S(1)}) custom-call(s32[2,8]{1,0:T(2,128)S(1)} %compare_select_fusion.1.target_ref, bf16[512,256]{1,0:T(8,128)(2,1)S(1)} %get-tuple-element.25.own_ref, bf16[512,256]{1,0:T(8,128)(2,1)S(1)} %collective-permute-done.2.pair_ref, bf16[512,256]{1,0:T(8,128)(2,1)S(1)} %collective-permute-done.3.cross_ref, ...), custom_call_target="tpu_custom_call" | custom-call | tf_op jit(solution)/shard_map/sweep/pallas_call | solution.py:172
  25.5 3.6 %collective-permute-start.5 = (bf16[512,256]{1,0:T(8,128)(2,1)S(1)}, bf16[512,256]{1,0:T(8,128)(2,1)S(1)}, u32[]{:S(2)}, u32[]{:S(2)}) collective-permute-start(bf16[512,256]{1,0:T(8,128)(2,1)S(1)} %get-tuple-element.27.own_ref), channel_id=1, source_target_pairs={{1,2},{2,1},{3,4},{4,3},{5,6},{6,5},{7,8},{8,7},{9,10},{10,9},{11,... | collective-permute-start | bytes 786440 | tf_op jit(solution)/shard_map/ppermute | solution.py:345
  29.2 0.1 collective-permute-start.4
  29.3 0.3 projected.4._.refs_2_
  29.6 3.6 %collective-permute-done.5.cross_ref = bf16[512,256]{1,0:T(8,128)(2,1)S(1)} collective-permute-done((bf16[512,256]{1,0:T(8,128)(2,1)S(1)}, bf16[512,256]{1,0:T(8,128)(2,1)S(1)}, u32[]{:S(2)}, u32[]{:S(2)}) %collective-permute-start.5) | collective-permute-done | bytes 262176 | tf_op jit(solution)/shard_map/ppermute | solution.py:345
  33.2 0.0 collective-permute-done.4.pair_ref
  33.2 2.5 %sweep.6 = (f32[512,256]{1,0:T(8,128)S(1)}, bf16[512,256]{1,0:T(8,128)(2,1)S(1)}) custom-call(s32[2,8]{1,0:T(2,128)S(1)} %compare_select_fusion.1.target_ref, bf16[512,256]{1,0:T(8,128)(2,1)S(1)} %get-tuple-element.27.own_ref, bf16[512,256]{1,0:T(8,128)(2,1)S(1)} %collective-permute-done.4.pair_ref, bf16[512,256]{1,0:T(8,128)(2,1)S(1)} %collective-permute-done.5.cross_ref, ...), custom_call_target="tpu_custom_call" | custom-call | tf_op jit(solution)/shard_map/sweep/pallas_call | solution.py:172
  35.7 3.6 %collective-permute-start.7 = (bf16[512,256]{1,0:T(8,128)(2,1)S(1)}, bf16[512,256]{1,0:T(8,128)(2,1)S(1)}, u32[]{:S(2)}, u32[]{:S(2)}) collective-permute-start(bf16[512,256]{1,0:T(8,128)(2,1)S(1)} %get-tuple-element.29.own_ref), channel_id=1, source_target_pairs={{1,2},{2,1},{3,4},{4,3},{5,6},{6,5},{7,8},{8,7},{9,10},{10,9},{11,... | collective-permute-start | bytes 786440 | tf_op jit(solution)/shard_map/ppermute | solution.py:345
  39.4 0.1 collective-permute-start.6
  39.5 0.3 projected.5._.refs_3_
  39.8 3.6 %collective-permute-done.7.cross_ref = bf16[512,256]{1,0:T(8,128)(2,1)S(1)} collective-permute-done((bf16[512,256]{1,0:T(8,128)(2,1)S(1)}, bf16[512,256]{1,0:T(8,128)(2,1)S(1)}, u32[]{:S(2)}, u32[]{:S(2)}) %collective-permute-start.7) | collective-permute-done | bytes 262176 | tf_op jit(solution)/shard_map/ppermute | solution.py:345
  43.4 0.0 collective-permute-done.6.pair_ref
  43.4 3.2 %sweep.7 = (f32[512,256]{1,0:T(8,128)S(1)}, bf16[512,256]{1,0:T(8,128)(2,1)}) custom-call(s32[2,8]{1,0:T(2,128)S(1)} %compare_select_fusion.1.target_ref, bf16[512,256]{1,0:T(8,128)(2,1)S(1)} %get-tuple-element.29.own_ref, bf16[512,256]{1,0:T(8,128)(2,1)S(1)} %collective-permute-done.6.pair_ref, bf16[512,256]{1,0:T(8,128)(2,1)S(1)} %collective-permute-done.7.cross_ref, ...), custom_call_target="tpu_custom_call" | custom-call | tf_op jit(solution)/shard_map/sweep/pallas_call | solution.py:172
  46.6 0.3 packed.1
  46.9 33.6 %all_to_all.15.in_ref = bf16[32,48,128]{2,1,0:T(8,128)(2,1)S(1)} all-to-all(bf16[32,48,128]{2,1,0:T(8,128)(2,1)S(1)} %packed.1), channel_id=1, replica_groups=mesh['leaf_0'=8,'leaf_1'=4,'sib_0'=4,'sib_1'=2] {'leaf_1','sib_0','sib_1'}, dimensions={0} | all-to-all | bytes 786432 | tf_op jit(solution)/shard_map/all_to_all | solution.py:323
  80.5 0.1 added.1
  80.5 19.8 %all_to_all.16.in_ref = f32[8,40,128]{2,1,0:T(8,128)S(1)} all-to-all(f32[8,40,128]{2,1,0:T(8,128)S(1)} %added.1), channel_id=1, replica_groups=mesh['leaf_0'=8,'leaf_1'=4,'sib_0'=4,'sib_1'=2] {'leaf_0'}, dimensions={0} | all-to-all | bytes 327680 | tf_op jit(solution)/shard_map/all_to_all | solution.py:323
  100.4 14.6 %all_to_all.17.arrived_ref = bf16[32,48,128]{2,1,0:T(8,128)(2,1)S(1)} all-to-all(bf16[32,48,128]{2,1,0:T(8,128)(2,1)S(1)} %split.1), channel_id=1, replica_groups=mesh['leaf_0'=8,'leaf_1'=4,'sib_0'=4,'sib_1'=2] {'leaf_1','sib_0','sib_1'}, dimensions={0} | all-to-all | bytes 786432 | tf_op jit(solution)/shard_map/all_to_all | solution.py:323
  114.9 9.1 %last_step.1 = (f32[512,128]{1,0:T(8,128)}, f32[128,128]{1,0:T(8,128)}) custom-call(bf16[32,48,128]{2,1,0:T(8,128)(2,1)S(1)} %all_to_all.17.arrived_ref, f32[512,256]{1,0:T(8,128)S(1)} %get-tuple-element.17.basis_ref.refs_0_, f32[512,256]{1,0:T(8,128)S(1)} %get-tuple-element.26.value_ref.refs_1_, f32[512,256]{1,0:T(8,128)S(1)} %get-tuple-element.28.value_ref.refs_2_, ...), custom_call_target="tpu_custom_call" | custom-call | tf_op jit(solution)/shard_map/last_step/pallas_call | solution.py:313
  (5 shorter events, 0.1 us)
Async XLA Ops:
  0.6 7.5 %copy-start = (f32[512,128]{1,0:T(8,128)S(1)}, f32[512,128]{1,0:T(8,128)}, u32[]{:S(2)}) copy-start(f32[512,128]{1,0:T(8,128)} %factor_ref.1) | copy-start | bytes 786436
  0.6 7.8 %copy-start.1 = (s32[2,8]{1,0:T(2,128)S(1)}, s32[2,8]{1,0:T(2,128)}, u32[]{:S(2)}) copy-start(s32[2,8]{1,0:T(2,128)} %param.11) | copy-start | bytes 196
  3.4 8.9 %collective-permute-start.1 = (bf16[512,256]{1,0:T(8,128)(2,1)}, bf16[512,256]{1,0:T(8,128)(2,1)}, u32[]{:S(2)}, u32[]{:S(2)}) collective-permute-start(bf16[512,256]{1,0:T(8,128)(2,1)} %get-tuple-element.20.own_ref), channel_id=1, source_target_pairs={{1,2},{2,1},{3,4},{4,3},{5,6},{6,5},{7,8},{8,7},{9,10},{10,9},{11,... | collective-permute-start | bytes 786440 | tf_op jit(solution)/shard_map/ppermute | solution.py:345
  8.0 4.4 %collective-permute-start = (bf16[512,256]{1,0:T(8,128)(2,1)}, bf16[512,256]{1,0:T(8,128)(2,1)}, u32[]{:S(2)}, u32[]{:S(2)}) collective-permute-start(bf16[512,256]{1,0:T(8,128)(2,1)} %get-tuple-element.20.own_ref), channel_id=1, source_target_pairs={{0,1},{1,0},{2,3},{3,2},{4,5},{5,4},{6,7},{7,6},{8,9},{9,8},{10,11... | collective-permute-start | bytes 786440 | tf_op jit(solution)/shard_map/ppermute | solution.py:346
  15.4 7.7 %collective-permute-start.3 = (bf16[512,256]{1,0:T(8,128)(2,1)S(1)}, bf16[512,256]{1,0:T(8,128)(2,1)S(1)}, u32[]{:S(2)}, u32[]{:S(2)}) collective-permute-start(bf16[512,256]{1,0:T(8,128)(2,1)S(1)} %get-tuple-element.25.own_ref), channel_id=1, source_target_pairs={{1,2},{2,1},{3,4},{4,3},{5,6},{6,5},{7,8},{8,7},{9,10},{10,9},{11,... | collective-permute-start | bytes 786440 | tf_op jit(solution)/shard_map/ppermute | solution.py:345
  19.0 4.0 %collective-permute-start.2 = (bf16[512,256]{1,0:T(8,128)(2,1)S(1)}, bf16[512,256]{1,0:T(8,128)(2,1)S(1)}, u32[]{:S(2)}, u32[]{:S(2)}) collective-permute-start(bf16[512,256]{1,0:T(8,128)(2,1)S(1)} %get-tuple-element.25.own_ref), channel_id=1, source_target_pairs={{0,1},{1,0},{2,3},{3,2},{4,5},{5,4},{6,7},{7,6},{8,9},{9,8},{10,11... | collective-permute-start | bytes 786440 | tf_op jit(solution)/shard_map/ppermute | solution.py:346
  25.5 7.7 %collective-permute-start.5 = (bf16[512,256]{1,0:T(8,128)(2,1)S(1)}, bf16[512,256]{1,0:T(8,128)(2,1)S(1)}, u32[]{:S(2)}, u32[]{:S(2)}) collective-permute-start(bf16[512,256]{1,0:T(8,128)(2,1)S(1)} %get-tuple-element.27.own_ref), channel_id=1, source_target_pairs={{1,2},{2,1},{3,4},{4,3},{5,6},{6,5},{7,8},{8,7},{9,10},{10,9},{11,... | collective-permute-start | bytes 786440 | tf_op jit(solution)/shard_map/ppermute | solution.py:345
  29.2 4.0 %collective-permute-start.4 = (bf16[512,256]{1,0:T(8,128)(2,1)S(1)}, bf16[512,256]{1,0:T(8,128)(2,1)S(1)}, u32[]{:S(2)}, u32[]{:S(2)}) collective-permute-start(bf16[512,256]{1,0:T(8,128)(2,1)S(1)} %get-tuple-element.27.own_ref), channel_id=1, source_target_pairs={{0,1},{1,0},{2,3},{3,2},{4,5},{5,4},{6,7},{7,6},{8,9},{9,8},{10,11... | collective-permute-start | bytes 786440 | tf_op jit(solution)/shard_map/ppermute | solution.py:346
  35.7 7.7 %collective-permute-start.7 = (bf16[512,256]{1,0:T(8,128)(2,1)S(1)}, bf16[512,256]{1,0:T(8,128)(2,1)S(1)}, u32[]{:S(2)}, u32[]{:S(2)}) collective-permute-start(bf16[512,256]{1,0:T(8,128)(2,1)S(1)} %get-tuple-element.29.own_ref), channel_id=1, source_target_pairs={{1,2},{2,1},{3,4},{4,3},{5,6},{6,5},{7,8},{8,7},{9,10},{10,9},{11,... | collective-permute-start | bytes 786440 | tf_op jit(solution)/shard_map/ppermute | solution.py:345
  39.4 4.0 %collective-permute-start.6 = (bf16[512,256]{1,0:T(8,128)(2,1)S(1)}, bf16[512,256]{1,0:T(8,128)(2,1)S(1)}, u32[]{:S(2)}, u32[]{:S(2)}) collective-permute-start(bf16[512,256]{1,0:T(8,128)(2,1)S(1)} %get-tuple-element.29.own_ref), channel_id=1, source_target_pairs={{0,1},{1,0},{2,3},{3,2},{4,5},{5,4},{6,7},{7,6},{8,9},{9,8},{10,11... | collective-permute-start | bytes 786440 | tf_op jit(solution)/shard_map/ppermute | solution.py:346

commit v2 on v1

--- a/solution.py
+++ b/solution.py
@@ -1,3 +1,5 @@
+import functools
+
 import jax
 import jax.numpy as jnp
 from jax import lax
@@ -119,21 +121,49 @@
     )(*(pltpu.with_memory_space_constraint(v, pltpu.HBM) for v in (order, sources, inverse, factor, near)))
 
 
-def turn_kernel(factor_ref, basis_ref, high_ref, low_ref, sum_ref):
+def turn_kernel(
+    target_ref, factor_ref, basis_ref, near_ref,
+    high_ref, low_ref, sum_ref, own_ref, pair_ref, cross_ref, total,
+):
+    leaves, near, size, _ = near_ref.shape
+    columns = basis_ref.shape[1] - factor_ref.shape[1]
+    rank = factor_ref.shape[1]
     factor_high, factor_low = parts(factor_ref[...])
     high_ref[...] = factor_high.T
     low_ref[...] = factor_low.T
     sum_ref[...] = dot3((high_ref[...], low_ref[...]), parts(basis_ref[...]))
-
-
-def turned(factor, basis):
+    total[...] = jnp.zeros_like(total)
+    for leaf in range(leaves):
+        lifted = basis_ref[leaf * size : (leaf + 1) * size, columns:].astype(BF16).T
+        for k in range(near):
+            total[target_ref[leaf, k]] += dot(lifted, near_ref[leaf, k])
+    for leaf in range(leaves):
+        here = slice(leaf * rank, (leaf + 1) * rank)
+        pair_ref[here, :] = total[leaf].astype(BF16)
+        own_ref[here, :] = total[leaves + leaf]
+        cross_ref[here, :] = total[2 * leaves + leaf].astype(BF16)
+
+
+def turned(targets, factor, basis, near):
     rows, rank = factor.shape
+    leaves, size = near.shape[0], near.shape[2]
+    back = (leaves * rank, size)
     return pl.pallas_call(
         turn_kernel,
-        out_shape=(shape((rank, rows), BF16), shape((rank, rows), BF16), shape((rank, basis.shape[1]))),
+        out_shape=(
+            shape((rank, rows), BF16),
+            shape((rank, rows), BF16),
+            shape((rank, basis.shape[1])),
+            shape(back),
+            shape(back, BF16),
+            shape(back, BF16),
+        ),
+        in_specs=[SMEM] + [VMEM] * 3,
+        out_specs=(VMEM,) * 6,
+        scratch_shapes=[pltpu.VMEM((3 * leaves, rank, size), F32)],
         compiler_params=params(),
         name="turned",
-    )(factor, basis)
+    )(targets, factor, basis, near)
 
 
 def project_kernel(high_ref, low_ref, value_ref, sum_ref):
@@ -149,14 +179,38 @@
     )(high, low, value)
 
 
-def sweep_kernel(
-    target_ref, own_ref, pair_ref, cross_ref, near_ref, high_ref, low_ref, basis_ref, _,
-    next_ref, sent_ref, window,
-):
+def last_sweep_kernel(arrived_ref, *refs):
+    added_ref, window = refs[-2], refs[-1]
+    sweep_kernel(0, *refs[:8], None, refs[8], window)
+    total = arrived_ref[0].astype(F32)
+    for i in range(1, arrived_ref.shape[0]):
+        total += arrived_ref[i].astype(F32)
+    total = jnp.concatenate([total[:TILE] + total[TILE : 2 * TILE], total[2 * TILE :]], axis=0)
+    for i in range(added_ref.shape[0]):
+        added_ref[i] = total
+
+
+def last_sweep(arrived, count, targets, own, pair, cross, near, high, low, basis):
+    leaves, size = near.shape[0], near.shape[2]
+    return pl.pallas_call(
+        last_sweep_kernel,
+        out_shape=(shape(basis.shape), shape((count, arrived.shape[1] - TILE, LANES))),
+        in_specs=[VMEM, SMEM] + [VMEM] * 7,
+        out_specs=(VMEM, VMEM),
+        scratch_shapes=[pltpu.VMEM((3 * leaves, size, basis.shape[1]), BF16)],
+        compiler_params=params(),
+        name="last_sweep",
+    )(arrived, targets, own, pair, cross, near, high, low, basis)
+
+
+def sweep_kernel(extras, target_ref, own_ref, pair_ref, cross_ref, near_ref, high_ref, low_ref, basis_ref, *refs):
+    extra_refs, next_ref, sent_refs, window = refs[1 : 1 + extras], refs[1 + extras], refs[2 + extras : -1], refs[-1]
     leaves, near, size, _ = near_ref.shape
     for place, ref in enumerate((pair_ref, own_ref, cross_ref)):
         for leaf in range(leaves):
             window[place * leaves + leaf] = ref[leaf * size : (leaf + 1) * size, :]
+    for extra_ref, sent_ref in zip(extra_refs, sent_refs):
+        sent_ref[leaves * size :, :] = extra_ref[...]
     for leaf in range(leaves):
         here = pl.ds(leaf * size, size)
         image = dot(near_ref[leaf, 0], window[target_ref[leaf, 0]])
@@ -164,20 +218,23 @@
             image += dot(near_ref[leaf, k], window[target_ref[leaf, k]])
         value = basis_ref[here, :] - dot3((high_ref[leaf], low_ref[leaf]), parts(image))
         next_ref[here, :] = value
-        sent_ref[here, :] = value.astype(BF16)
-
-
-def sweep(targets, own, pair, cross, near, high, low, basis, sums):
+        for sent_ref in sent_refs:
+            sent_ref[here, :] = value.astype(BF16)
+
+
+def sweep(targets, own, pair, cross, near, high, low, basis, after, extras, sends):
     leaves, size = near.shape[0], near.shape[2]
-    return pl.pallas_call(
-        sweep_kernel,
-        out_shape=(shape(basis.shape), shape(basis.shape, BF16)),
-        in_specs=[SMEM] + [VMEM] * 7 + [ANY],
-        out_specs=(VMEM, VMEM),
-        scratch_shapes=[pltpu.VMEM((3 * leaves, size, basis.shape[1]), BF16)],
+    rows, width = basis.shape
+    sent = shape((rows + (extras[0].shape[0] if extras else 0), width), BF16)
+    return pl.pallas_call(
+        functools.partial(sweep_kernel, len(extras)),
+        out_shape=(shape(basis.shape),) + (sent,) * sends,
+        in_specs=[SMEM] + [VMEM] * 7 + [ANY] + [VMEM] * len(extras),
+        out_specs=(VMEM,) * (1 + sends),
+        scratch_shapes=[pltpu.VMEM((3 * leaves, size, width), BF16)],
         compiler_params=params(),
         name="sweep",
-    )(targets, own, pair, cross, near, high, low, basis, sums)
+    )(targets, own, pair, cross, near, high, low, basis, after, *extras)
 
 
 def place_of(chunk, rank):
@@ -185,11 +242,21 @@
     return slice(rest, rest + TILE), slice(half * LANES, half * LANES + LANES)
 
 
-def pack_kernel(high_ref, low_ref, value_ref, *refs):
-    sum_refs, (out_ref, changes) = refs[:ITERS], refs[ITERS:]
+def pack_kernel(high_ref, low_ref, value_ref, sent_ref, own_ref, pair_ref, cross_ref, *refs):
+    sum_refs, (out_ref, changes) = refs[: ITERS - 1], refs[ITERS - 1 :]
     rank = changes.shape[1]
+    size = own_ref.shape[1]
+    leaves = own_ref.shape[0] // rank
     sums = [ref[...] for ref in sum_refs]
     sums.append(dot3((high_ref[...], low_ref[...]), parts(value_ref[...])))
+    final = sums[0]
+    for leaf in range(leaves):
+        here = slice(leaf * rank, (leaf + 1) * rank)
+        there = slice(leaves * size + leaf * rank, leaves * size + (leaf + 1) * rank)
+        back_high, back_low = parts(own_ref[here, :] + pair_ref[there, :].astype(F32) + cross_ref[there, :].astype(F32))
+        sent = sent_ref[leaf * size : (leaf + 1) * size, :]
+        final -= dot(back_high, sent) + dot(back_low, sent)
+    sums.append(final)
     start = sums[0].astype(BF16).astype(F32)
     changes[0] = start
     changes[1] = sums[0] - start
@@ -202,7 +269,7 @@
             out_ref[chunk, j * TILE : (j + 2) * TILE, :] = both.astype(BF16)
 
 
-def packed(high, low, value, sums, count):
+def packed(high, low, value, sent, back, sums, count):
     rank, width = sums[0].shape
     return pl.pallas_call(
         pack_kernel,
@@ -210,25 +277,7 @@
         scratch_shapes=[pltpu.VMEM((LEVELS + 1, rank, width), F32)],
         compiler_params=params(),
         name="packed",
-    )(high, low, value, *sums)
-
-
-def add_kernel(in_ref, out_ref):
-    total = in_ref[0].astype(F32)
-    for i in range(1, in_ref.shape[0]):
-        total += in_ref[i].astype(F32)
-    total = jnp.concatenate([total[:TILE] + total[TILE : 2 * TILE], total[2 * TILE :]], axis=0)
-    for i in range(out_ref.shape[0]):
-        out_ref[i] = total
-
-
-def added(arrived, count):
-    return pl.pallas_call(
-        add_kernel,
-        out_shape=shape((count, arrived.shape[1] - TILE, LANES)),
-        compiler_params=params(),
-        name="added",
-    )(arrived)
+    )(high, low, value, sent, *back, *sums)
 
 
 def split_kernel(in_ref, out_ref):
@@ -340,20 +389,32 @@
     basis, sent, inverse_high, inverse_low, near = first_step(
         ordering.reshape(1, -1), sources, inverse, low_rank, nearby_blocks
     )
+    plane, line = lax.axis_size(PLANE), lax.axis_size(LINE)
     bases, sums = [basis], []
+    own = to_pair = to_cross = sent
     for k in range(ITERS):
-        cross = lax.ppermute(sent, AXES, across)
-        pair = lax.ppermute(sent, AXES, within)
+        cross = lax.ppermute(to_cross, AXES, across)
+        pair = lax.ppermute(to_pair, AXES, within)
+        if k == ITERS - 1:
+            break
+        extras = ()
         if k == 0:
-            high, low, latest = turned(low_rank, basis)
+            high, low, after, back_own, *extras = turned(targets, low_rank, basis, near)
         else:
-            latest = projected(high, low, bases[-1])
-        sums.append(latest)
-        value, sent = sweep(targets, sent, pair, cross, near, inverse_high, inverse_low, basis, latest)
+            after = projected(high, low, bases[-1])
+        if k == 1:
+            back = (back_own, pair, cross)
+        sums.append(after)
+        value, *sent = sweep(
+            targets, own, pair, cross, near, inverse_high, inverse_low, basis, after, extras, 1 if k else 2
+        )
         bases.append(value)
-    plane, line = lax.axis_size(PLANE), lax.axis_size(LINE)
-    arrived = exchanged(packed(high, low, bases[-1], sums, plane), PLANE)
-    arrived = exchanged(added(arrived, line), LINE)
+        own = to_pair = sent[0]
+        to_cross = sent[-1]
+    arrived = exchanged(packed(high, low, bases[-1], own, back, sums, plane), PLANE)
+    value, after = last_sweep(arrived, line, targets, own, pair, cross, near, inverse_high, inverse_low, basis)
+    bases.append(value)
+    arrived = exchanged(after, LINE)
     arrived = exchanged(split(arrived, plane), PLANE)
     return last_step(arrived, bases, low_rank.shape[1])
 

time: 124 us -> 123 us (level)
  blocking collectives: 68 us -> 37.1 us
  starting transfers between devices: 15.9 us -> 35.1 us
  local copies, waits for them, and re-layouts: 0.01 us -> 7.39 us
  waiting for transfers between devices: 14.8 us -> 17.5 us
    all_to_all x3 -> x2, blocking collectives: 68 us -> 37.1 us  [exchanged(): return lax.all_to_all(array, axes, 0, 0, tiled=True)]
    all_to_all x0 -> x1, starting transfers between devices: none -> 19.3 us  [exchanged(): return lax.all_to_all(array, axes, 0, 0, tiled=True)]
    unnamed x4 -> x30, local copies, waits for them, and re-layouts: 0.01 us -> 7.39 us
    ppermute x8, waiting for transfers between devices: 14.8 us -> 17.5 us  [the longest x4 17.5 us: on_device(): cross = lax.ppermute(to_cross, AXES, across)]
    pallas_call x5 -> x4, Pallas kernels: 11.2 us -> 10.4 us  [the longest x3 7.98 us: sweep(): pl.pallas_call(functools.partial(sweep_kernel, len(extras)), out_shape=(s...]
  transfers between devices with their start and end apart: 8 -> 9, of which waited for: 4 -> 4; matrix products, arithmetic and copies ran while one was open for 0% -> 0% of each run, Pallas kernels for 1% -> 1%
where the time goes in v2:
time: 123 us; the launch traced here: 122 us
  blocking collectives  37.1 us (30%)
  starting transfers between devices  35.1 us (29%)
  Pallas kernels  24.4 us (20%)
  waiting for transfers between devices  17.5 us (14%)
  local copies, waits for them, and re-layouts  7.39 us (6%)
    all_to_all x2, blocking collectives, exchanged(): return lax.all_to_all(array, axes, 0, 0, tiled=True)  37.1 us
    all_to_all x1, starting transfers between devices, exchanged(): return lax.all_to_all(array, axes, 0, 0, tiled=True)  19.3 us
    ppermute x4, waiting for transfers between devices, on_device(): cross = lax.ppermute(to_cross, AXES, across)  17.5 us
    ppermute x4, starting transfers between devices, on_device(): cross = lax.ppermute(to_cross, AXES, across)  15.4 us
    pallas_call x1, Pallas kernels, last_step(): pl.pallas_call(last_kernel, out_shape=(shape((rows, width - rank)), shape...  9.07 us
    pallas_call x3, Pallas kernels, sweep(): pl.pallas_call(functools.partial(sweep_kernel, len(extras)), out_shape=(s...  7.98 us
    unnamed x30, local copies, waits for them, and re-layouts  7.39 us
    pallas_call x1, Pallas kernels, first_step(): pl.pallas_call(first_kernel, out_shape=(shape((rows, width)), shape((rows...  2.72 us
  transfers between devices with their start and end apart: 9, of which 4 were waited for; matrix products, arithmetic and copies ran while one was open for 0% of the time, Pallas kernels for 1%

profile of v2, /device:TPU:1, one launch (start us, length us, event | category | flops | bytes accessed | tf_op | source)
XLA Modules:
  0.0 122.3 jit_solution(8534649082611368451)
XLA Ops:
  0.7 2.7 %first_step.1 = (f32[512,256]{1,0:T(8,128)S(1)}, bf16[512,256]{1,0:T(8,128)(2,1)}, bf16[2,256,256]{2,1,0:T(8,128)(2,1)S(1)}, bf16[2,256,256]{2,1,0:T(8,128)(2,1)S(1)}, bf16[2,8,256,256]{3,2,1,0:T(8,128)(2,1)S(1)}) custom-call(s32[1,512]{1,0:T(1,128)} %bitcast.1, f32[512,128]{1,0:T(8,128)} %source_hbm.1, f32[2,256,256]{2,1,0:T(8,128)} %inverse_hbm.1, ...), custom_call_target="tpu_custom_call" | custom-call | tf_op jit(solution)/shard_map/first_step/pallas_call | solution.py:101
  3.4 4.6 %collective-permute-start.1 = (bf16[512,256]{1,0:T(8,128)(2,1)}, bf16[512,256]{1,0:T(8,128)(2,1)}, u32[]{:S(2)}, u32[]{:S(2)}) collective-permute-start(bf16[512,256]{1,0:T(8,128)(2,1)} %get-tuple-element.26.own_ref), channel_id=1, source_target_pairs={{1,2},{2,1},{3,4},{4,3},{5,6},{6,5},{7,8},{8,7},{9,10},{10,9},{11,... | collective-permute-start | bytes 786440 | tf_op jit(solution)/shard_map/ppermute | solution.py:396
  8.0 0.1 collective-permute-start
  8.1 1.2 turned.1
  9.4 3.0 %collective-permute-done.1.cross_ref = bf16[512,256]{1,0:T(8,128)(2,1)} collective-permute-done((bf16[512,256]{1,0:T(8,128)(2,1)}, bf16[512,256]{1,0:T(8,128)(2,1)}, u32[]{:S(2)}, u32[]{:S(2)}) %collective-permute-start.1) | collective-permute-done | bytes 262176 | tf_op jit(solution)/shard_map/ppermute | solution.py:396
  12.3 3.0 %sweep.3 = (f32[512,256]{1,0:T(8,128)S(1)}, bf16[768,256]{1,0:T(8,128)(2,1)S(1)}, bf16[768,256]{1,0:T(8,128)(2,1)S(1)}) custom-call(s32[2,8]{1,0:T(2,128)S(1)} %compare_select_fusion.1.target_ref.refs_0_, bf16[512,256]{1,0:T(8,128)(2,1)} %get-tuple-element.26.own_ref, bf16[512,256]{1,0:T(8,128)(2,1)} %collective-permute-done.pair_ref, ...), custom_call_target="tpu_custom_call" | custom-call | tf_op jit(solution)/shard_map/sweep/pallas_call | solution.py:229
  15.4 3.6 %collective-permute-start.3 = (bf16[768,256]{1,0:T(8,128)(2,1)S(1)}, bf16[768,256]{1,0:T(8,128)(2,1)S(1)}, u32[]{:S(2)}, u32[]{:S(2)}) collective-permute-start(bf16[768,256]{1,0:T(8,128)(2,1)S(1)} %get-tuple-element.33), channel_id=1, source_target_pairs={{1,2},{2,1},{3,4},{4,3},{5,6},{6,5},{7,8},{8,7},{9,10},{10,9},{11,... | collective-permute-start | bytes 1179656 | tf_op jit(solution)/shard_map/ppermute | solution.py:396
  19.0 0.1 collective-permute-start.2
  19.1 0.3 projected.2.refs_0_.refs_1_
  19.4 0.8 copy-done
  20.3 4.2 %collective-permute-done.3.cross_ref = bf16[768,256]{1,0:T(8,128)(2,1)S(1)} collective-permute-done((bf16[768,256]{1,0:T(8,128)(2,1)S(1)}, bf16[768,256]{1,0:T(8,128)(2,1)S(1)}, u32[]{:S(2)}, u32[]{:S(2)}) %collective-permute-start.3) | collective-permute-done | bytes 393248 | tf_op jit(solution)/shard_map/ppermute | solution.py:396
  24.5 2.5 %sweep.4 = (f32[512,256]{1,0:T(8,128)S(1)}, bf16[512,256]{1,0:T(8,128)(2,1)S(1)}) custom-call(s32[2,8]{1,0:T(2,128)S(1)} %compare_select_fusion.1.target_ref.refs_0_, bf16[768,256]{1,0:T(8,128)(2,1)S(1)} %get-tuple-element.32.own_ref, bf16[768,256]{1,0:T(8,128)(2,1)S(1)} %collective-permute-done.2.pair_ref, ...), custom_call_target="tpu_custom_call" | custom-call | tf_op jit(solution)/shard_map/sweep/pallas_call | solution.py:229
  27.0 3.6 %collective-permute-start.5 = (bf16[512,256]{1,0:T(8,128)(2,1)S(1)}, bf16[512,256]{1,0:T(8,128)(2,1)S(1)}, u32[]{:S(2)}, u32[]{:S(2)}) collective-permute-start(bf16[512,256]{1,0:T(8,128)(2,1)S(1)} %get-tuple-element.35.own_ref), channel_id=1, source_target_pairs={{1,2},{2,1},{3,4},{4,3},{5,6},{6,5},{7,8},{8,7},{9,10},{10,9},{11,... | collective-permute-start | bytes 786440 | tf_op jit(solution)/shard_map/ppermute | solution.py:396
  30.7 0.3 projected.3.refs_0_.refs_2_
  31.0 3.6 %collective-permute-done.5.cross_ref = bf16[512,256]{1,0:T(8,128)(2,1)S(1)} collective-permute-done((bf16[512,256]{1,0:T(8,128)(2,1)S(1)}, bf16[512,256]{1,0:T(8,128)(2,1)S(1)}, u32[]{:S(2)}, u32[]{:S(2)}) %collective-permute-start.5) | collective-permute-done | bytes 262176 | tf_op jit(solution)/shard_map/ppermute | solution.py:396
  34.7 2.5 %sweep.5 = (f32[512,256]{1,0:T(8,128)S(1)}, bf16[512,256]{1,0:T(8,128)(2,1)S(1)}) custom-call(s32[2,8]{1,0:T(2,128)S(1)} %compare_select_fusion.1.target_ref.refs_0_, bf16[512,256]{1,0:T(8,128)(2,1)S(1)} %get-tuple-element.35.own_ref, bf16[512,256]{1,0:T(8,128)(2,1)S(1)} %collective-permute-done.4.pair_ref, ...), custom_call_target="tpu_custom_call" | custom-call | tf_op jit(solution)/shard_map/sweep/pallas_call | solution.py:229
  37.2 0.4 packed.1
  37.5 0.8 copy-done.4
  38.4 0.8 copy-done.6
  39.1 0.7 copy-done.7
  39.8 19.3 %all-to-all-start = ((bf16[32,48,128]{2,1,0:T(8,128)(2,1)}), bf16[32,48,128]{2,1,0:T(8,128)(2,1)S(1)}, u32[]{:S(2)}, u32[]{:S(2)}) async-start(bf16[32,48,128]{2,1,0:T(8,128)(2,1)} %copy-done.6), calls=%async_computation | async-start | bytes 786432 | tf_op jit(solution)/shard_map/all_to_all | solution.py:372
  59.1 3.5 %collective-permute-start.7 = (bf16[512,256]{1,0:T(8,128)(2,1)}, bf16[512,256]{1,0:T(8,128)(2,1)S(1)}, u32[]{:S(2)}, u32[]{:S(2)}) collective-permute-start(bf16[512,256]{1,0:T(8,128)(2,1)} %copy-done.7), channel_id=1, source_target_pairs={{1,2},{2,1},{3,4},{4,3},{5,6},{6,5},{7,8},{8,7},{9,10},{10,9},{11,... | collective-permute-start | bytes 786440 | tf_op jit(solution)/shard_map/ppermute | solution.py:396
  62.8 6.6 %collective-permute-done.7.refs_3_ = bf16[512,256]{1,0:T(8,128)(2,1)S(1)} collective-permute-done((bf16[512,256]{1,0:T(8,128)(2,1)}, bf16[512,256]{1,0:T(8,128)(2,1)S(1)}, u32[]{:S(2)}, u32[]{:S(2)}) %collective-permute-start.7) | collective-permute-done | bytes 262176 | tf_op jit(solution)/shard_map/ppermute | solution.py:396
  69.4 0.7 copy-done.10
  70.1 0.7 copy-done.12
  70.8 0.9 copy-done.8
  71.8 0.9 copy-done.11
  72.7 0.9 copy-done.13
  73.7 2.5 %last_sweep.1 = (f32[512,256]{1,0:T(8,128)S(1)}, f32[8,40,128]{2,1,0:T(8,128)S(1)}) custom-call(bf16[32,48,128]{2,1,0:T(8,128)(2,1)S(1)} %all-to-all-done.arrived_ref, s32[2,8]{1,0:T(2,128)S(1)} %compare_select_fusion.1.target_ref.refs_0_, bf16[512,256]{1,0:T(8,128)(2,1)S(1)} %copy-done.8, bf16[512,256]{1,0:T(8,128)(2,1)S(1)} %copy-done.13, ...), custom_call_target="tpu_custom_call" | custom-call | tf_op jit(solution)/shard_map/last_sweep/pallas_call | solution.py:195
  76.1 18.6 %all_to_all.15.in_ref = f32[8,40,128]{2,1,0:T(8,128)S(1)} all-to-all(f32[8,40,128]{2,1,0:T(8,128)S(1)} %get-tuple-element.40), channel_id=1, replica_groups=mesh['leaf_0'=8,'leaf_1'=4,'sib_0'=4,'sib_1'=2] {'leaf_0'}, dimensions={0} | all-to-all | bytes 327680 | tf_op jit(solution)/shard_map/all_to_all | solution.py:372
  94.8 18.5 %all_to_all.16.arrived_ref = bf16[32,48,128]{2,1,0:T(8,128)(2,1)S(1)} all-to-all(bf16[32,48,128]{2,1,0:T(8,128)(2,1)S(1)} %split.1), channel_id=1, replica_groups=mesh['leaf_0'=8,'leaf_1'=4,'sib_0'=4,'sib_1'=2] {'leaf_1','sib_0','sib_1'}, dimensions={0} | all-to-all | bytes 786432 | tf_op jit(solution)/shard_map/all_to_all | solution.py:372
  113.2 9.1 %last_step.1 = (f32[512,128]{1,0:T(8,128)}, f32[128,128]{1,0:T(8,128)}) custom-call(bf16[32,48,128]{2,1,0:T(8,128)(2,1)S(1)} %all_to_all.16.arrived_ref, f32[512,256]{1,0:T(8,128)S(1)} %get-tuple-element.22.basis_ref.refs_7_.refs_0_, f32[512,256]{1,0:T(8,128)S(1)} %copy-done.1, f32[512,256]{1,0:T(8,128)S(1)} %copy-done.3, f32[512,256]{1,0:T(8,128)S(1)} %copy-done.5, ...), custom_call_target="tpu_custom_call" | custom-call | tf_op jit(solution)/shard_map/last_step/pallas_call | solution.py:362
  (30 shorter events, 0.3 us)
Async XLA Ops:
  0.6 7.5 %copy-start.9 = (f32[512,128]{1,0:T(8,128)S(1)}, f32[512,128]{1,0:T(8,128)}, u32[]{:S(2)}) copy-start(f32[512,128]{1,0:T(8,128)} %factor_ref.1) | copy-start | bytes 786436
  0.6 7.5 %copy-start.14 = (s32[2,8]{1,0:T(2,128)S(1)}, s32[2,8]{1,0:T(2,128)}, u32[]{:S(2)}) copy-start(s32[2,8]{1,0:T(2,128)} %param.11) | copy-start | bytes 196
  3.4 8.9 %collective-permute-start.1 = (bf16[512,256]{1,0:T(8,128)(2,1)}, bf16[512,256]{1,0:T(8,128)(2,1)}, u32[]{:S(2)}, u32[]{:S(2)}) collective-permute-start(bf16[512,256]{1,0:T(8,128)(2,1)} %get-tuple-element.26.own_ref), channel_id=1, source_target_pairs={{1,2},{2,1},{3,4},{4,3},{5,6},{6,5},{7,8},{8,7},{9,10},{10,9},{11,... | collective-permute-start | bytes 786440 | tf_op jit(solution)/shard_map/ppermute | solution.py:396
  8.0 4.4 %collective-permute-start = (bf16[512,256]{1,0:T(8,128)(2,1)}, bf16[512,256]{1,0:T(8,128)(2,1)}, u32[]{:S(2)}, u32[]{:S(2)}) collective-permute-start(bf16[512,256]{1,0:T(8,128)(2,1)} %get-tuple-element.26.own_ref), channel_id=1, source_target_pairs={{0,1},{1,0},{2,3},{3,2},{4,5},{5,4},{6,7},{7,6},{8,9},{9,8},{10,11... | collective-permute-start | bytes 786440 | tf_op jit(solution)/shard_map/ppermute | solution.py:397
  15.4 9.1 %collective-permute-start.3 = (bf16[768,256]{1,0:T(8,128)(2,1)S(1)}, bf16[768,256]{1,0:T(8,128)(2,1)S(1)}, u32[]{:S(2)}, u32[]{:S(2)}) collective-permute-start(bf16[768,256]{1,0:T(8,128)(2,1)S(1)} %get-tuple-element.33), channel_id=1, source_target_pairs={{1,2},{2,1},{3,4},{4,3},{5,6},{6,5},{7,8},{8,7},{9,10},{10,9},{11,... | collective-permute-start | bytes 1179656 | tf_op jit(solution)/shard_map/ppermute | solution.py:396
  19.0 5.4 %collective-permute-start.2 = (bf16[768,256]{1,0:T(8,128)(2,1)S(1)}, bf16[768,256]{1,0:T(8,128)(2,1)S(1)}, u32[]{:S(2)}, u32[]{:S(2)}) collective-permute-start(bf16[768,256]{1,0:T(8,128)(2,1)S(1)} %get-tuple-element.32.own_ref), channel_id=1, source_target_pairs={{0,1},{1,0},{2,3},{3,2},{4,5},{5,4},{6,7},{7,6},{8,9},{9,8},{10,11... | collective-permute-start | bytes 1179656 | tf_op jit(solution)/shard_map/ppermute | solution.py:397
  19.4 0.8 copy-start
  27.0 10.2 %copy-start.2 = (f32[512,256]{1,0:T(8,128)}, f32[512,256]{1,0:T(8,128)S(1)}, u32[]{:S(2)}) copy-start(f32[512,256]{1,0:T(8,128)S(1)} %get-tuple-element.36.value_ref.refs_2_) | copy-start | bytes 1572868
  27.0 7.7 %collective-permute-start.5 = (bf16[512,256]{1,0:T(8,128)(2,1)S(1)}, bf16[512,256]{1,0:T(8,128)(2,1)S(1)}, u32[]{:S(2)}, u32[]{:S(2)}) collective-permute-start(bf16[512,256]{1,0:T(8,128)(2,1)S(1)} %get-tuple-element.35.own_ref), channel_id=1, source_target_pairs={{1,2},{2,1},{3,4},{4,3},{5,6},{6,5},{7,8},{8,7},{9,10},{10,9},{11,... | collective-permute-start | bytes 786440 | tf_op jit(solution)/shard_map/ppermute | solution.py:396
  30.6 4.0 %collective-permute-start.4 = (bf16[512,256]{1,0:T(8,128)(2,1)S(1)}, bf16[512,256]{1,0:T(8,128)(2,1)S(1)}, u32[]{:S(2)}, u32[]{:S(2)}) collective-permute-start(bf16[512,256]{1,0:T(8,128)(2,1)S(1)} %get-tuple-element.35.own_ref), channel_id=1, source_target_pairs={{0,1},{1,0},{2,3},{3,2},{4,5},{5,4},{6,7},{7,6},{8,9},{9,8},{10,11... | collective-permute-start | bytes 786440 | tf_op jit(solution)/shard_map/ppermute | solution.py:397
  37.5 0.8 copy-start.4
  38.4 0.8 copy-start.6
  39.1 0.7 copy-start.7
  39.8 31.0 %all-to-all-start = ((bf16[32,48,128]{2,1,0:T(8,128)(2,1)}), bf16[32,48,128]{2,1,0:T(8,128)(2,1)S(1)}, u32[]{:S(2)}, u32[]{:S(2)}) async-start(bf16[32,48,128]{2,1,0:T(8,128)(2,1)} %copy-done.6), calls=%async_computation | async-start | bytes 786432 | tf_op jit(solution)/shard_map/all_to_all | solution.py:372
  59.1 10.3 %collective-permute-start.7 = (bf16[512,256]{1,0:T(8,128)(2,1)}, bf16[512,256]{1,0:T(8,128)(2,1)S(1)}, u32[]{:S(2)}, u32[]{:S(2)}) collective-permute-start(bf16[512,256]{1,0:T(8,128)(2,1)} %copy-done.7), channel_id=1, source_target_pairs={{1,2},{2,1},{3,4},{4,3},{5,6},{6,5},{7,8},{8,7},{9,10},{10,9},{11,... | collective-permute-start | bytes 786440 | tf_op jit(solution)/shard_map/ppermute | solution.py:396
  62.7 7.4 %collective-permute-start.6 = (bf16[512,256]{1,0:T(8,128)(2,1)}, bf16[512,256]{1,0:T(8,128)(2,1)S(1)}, u32[]{:S(2)}, u32[]{:S(2)}) collective-permute-start(bf16[512,256]{1,0:T(8,128)(2,1)} %copy-done.7), channel_id=1, source_target_pairs={{0,1},{1,0},{2,3},{3,2},{4,5},{5,4},{6,7},{7,6},{8,9},{9,8},{10,11... | collective-permute-start | bytes 786440 | tf_op jit(solution)/shard_map/ppermute | solution.py:397
  69.4 0.7 copy-start.10
  70.1 0.7 copy-start.12
  70.8 1.0 copy-start.8
  71.8 0.9 copy-start.11
  72.7 0.9 copy-start.13
  73.7 39.6 %copy-start.1 = (f32[512,256]{1,0:T(8,128)S(1)}, f32[512,256]{1,0:T(8,128)}, u32[]{:S(2)}) copy-start(f32[512,256]{1,0:T(8,128)} %copy-done) | copy-start | bytes 1572868
  73.7 39.6 %copy-start.3 = (f32[512,256]{1,0:T(8,128)S(1)}, f32[512,256]{1,0:T(8,128)}, u32[]{:S(2)}) copy-start(f32[512,256]{1,0:T(8,128)} %copy-done.2) | copy-start | bytes 1572868
  73.7 39.6 %copy-start.5 = (f32[512,256]{1,0:T(8,128)S(1)}, f32[512,256]{1,0:T(8,128)}, u32[]{:S(2)}) copy-start(f32[512,256]{1,0:T(8,128)} %copy-done.4) | copy-start | bytes 1572868

commit v3 on v2

--- a/solution.py
+++ b/solution.py
@@ -179,28 +179,40 @@
     )(high, low, value)
 
 
-def last_sweep_kernel(arrived_ref, *refs):
+def add_kernel(in_ref, out_ref):
+    total = in_ref[0].astype(F32)
+    for i in range(1, in_ref.shape[0]):
+        total += in_ref[i].astype(F32)
+    out_ref[...] = jnp.concatenate([total[:TILE] + total[TILE : 2 * TILE], total[2 * TILE :]], axis=0)
+
+
+def added(arrived):
+    return pl.pallas_call(
+        add_kernel,
+        out_shape=shape((arrived.shape[1] - TILE, LANES)),
+        compiler_params=params(),
+        name="added",
+    )(arrived)
+
+
+def last_sweep_kernel(line_ref, *refs):
     added_ref, window = refs[-2], refs[-1]
     sweep_kernel(0, *refs[:8], None, refs[8], window)
-    total = arrived_ref[0].astype(F32)
-    for i in range(1, arrived_ref.shape[0]):
-        total += arrived_ref[i].astype(F32)
-    total = jnp.concatenate([total[:TILE] + total[TILE : 2 * TILE], total[2 * TILE :]], axis=0)
     for i in range(added_ref.shape[0]):
-        added_ref[i] = total
-
-
-def last_sweep(arrived, count, targets, own, pair, cross, near, high, low, basis):
+        added_ref[i] = line_ref[...]
+
+
+def last_sweep(line, count, targets, own, pair, cross, near, high, low, basis):
     leaves, size = near.shape[0], near.shape[2]
     return pl.pallas_call(
         last_sweep_kernel,
-        out_shape=(shape(basis.shape), shape((count, arrived.shape[1] - TILE, LANES))),
+        out_shape=(shape(basis.shape), shape((count, *line.shape))),
         in_specs=[VMEM, SMEM] + [VMEM] * 7,
         out_specs=(VMEM, VMEM),
         scratch_shapes=[pltpu.VMEM((3 * leaves, size, basis.shape[1]), BF16)],
         compiler_params=params(),
         name="last_sweep",
-    )(arrived, targets, own, pair, cross, near, high, low, basis)
+    )(line, targets, own, pair, cross, near, high, low, basis)
 
 
 def sweep_kernel(extras, target_ref, own_ref, pair_ref, cross_ref, near_ref, high_ref, low_ref, basis_ref, *refs):
@@ -411,8 +423,9 @@
         bases.append(value)
         own = to_pair = sent[0]
         to_cross = sent[-1]
-    arrived = exchanged(packed(high, low, bases[-1], own, back, sums, plane), PLANE)
-    value, after = last_sweep(arrived, line, targets, own, pair, cross, near, inverse_high, inverse_low, basis)
+    lines = packed(high, low, bases[-1], own, back, sums, plane)
+    arrived = exchanged(lines, PLANE)
+    value, after = last_sweep(added(arrived), line, targets, own, pair, cross, near, inverse_high, inverse_low, basis)
     bases.append(value)
     arrived = exchanged(after, LINE)
     arrived = exchanged(split(arrived, plane), PLANE)

time: 123 us -> 120 us (0.976)
  local copies, waits for them, and re-layouts: 7.39 us -> 4.16 us
    all_to_all x1, waiting for transfers between devices: 0.01 us -> 6.63 us  [exchanged(): return lax.all_to_all(array, axes, 0, 0, tiled=True)]
    ppermute x4, waiting for transfers between devices: 17.5 us -> 10.9 us  [on_device(): cross = lax.ppermute(to_cross, AXES, across)]
    unnamed x30 -> x22, local copies, waits for them, and re-layouts: 7.39 us -> 4.16 us
  transfers between devices with their start and end apart: 9 -> 9, of which waited for: 4 -> 4; matrix products, arithmetic and copies ran while one was open for 0% -> 0% of each run, Pallas kernels for 1% -> 2%
where the time goes in v3:
time: 120 us
  blocking collectives  36.9 us (31%)
  starting transfers between devices  35.1 us (29%)
  Pallas kernels  25 us (21%)
  waiting for transfers between devices  17.5 us (15%)
  local copies, waits for them, and re-layouts  4.16 us (3%)
    all_to_all x2, blocking collectives, exchanged(): return lax.all_to_all(array, axes, 0, 0, tiled=True)  36.9 us
    all_to_all x1, starting transfers between devices, exchanged(): return lax.all_to_all(array, axes, 0, 0, tiled=True)  19.3 us
    ppermute x4, starting transfers between devices, on_device(): cross = lax.ppermute(to_cross, AXES, across)  15.4 us
    ppermute x4, waiting for transfers between devices, on_device(): cross = lax.ppermute(to_cross, AXES, across)  10.9 us
    pallas_call x1, Pallas kernels, last_step(): pl.pallas_call(last_kernel, out_shape=(shape((rows, width - rank)), shape...  9.07 us
    pallas_call x3, Pallas kernels, sweep(): pl.pallas_call(functools.partial(sweep_kernel, len(extras)), out_shape=(s...  7.98 us
    all_to_all x1, waiting for transfers between devices, exchanged(): return lax.all_to_all(array, axes, 0, 0, tiled=True)  6.63 us
    unnamed x22, local copies, waits for them, and re-layouts  4.16 us
  transfers between devices with their start and end apart: 9, of which 4 were waited for; matrix products, arithmetic and copies ran while one was open for 0% of the time, Pallas kernels for 2%

profile of v3, /device:TPU:1, one launch (start us, length us, event | category | flops | bytes accessed | tf_op | source)
XLA Modules:
  0.0 119.6 jit_solution(2599262119229522366)
XLA Ops:
  0.7 2.7 %first_step.1 = (f32[512,256]{1,0:T(8,128)S(1)}, bf16[512,256]{1,0:T(8,128)(2,1)}, bf16[2,256,256]{2,1,0:T(8,128)(2,1)S(1)}, bf16[2,256,256]{2,1,0:T(8,128)(2,1)S(1)}, bf16[2,8,256,256]{3,2,1,0:T(8,128)(2,1)S(1)}) custom-call(s32[1,512]{1,0:T(1,128)} %bitcast.1, f32[512,128]{1,0:T(8,128)} %source_hbm.1, f32[2,256,256]{2,1,0:T(8,128)} %inverse_hbm.1, ...), custom_call_target="tpu_custom_call" | custom-call | tf_op jit(solution)/shard_map/first_step/pallas_call | solution.py:101
  3.4 4.6 %collective-permute-start.1 = (bf16[512,256]{1,0:T(8,128)(2,1)}, bf16[512,256]{1,0:T(8,128)(2,1)}, u32[]{:S(2)}, u32[]{:S(2)}) collective-permute-start(bf16[512,256]{1,0:T(8,128)(2,1)} %get-tuple-element.26.own_ref), channel_id=1, source_target_pairs={{1,2},{2,1},{3,4},{4,3},{5,6},{6,5},{7,8},{8,7},{9,10},{10,9},{11,... | collective-permute-start | bytes 786440 | tf_op jit(solution)/shard_map/ppermute | solution.py:408
  8.0 0.1 collective-permute-start
  8.1 1.2 %turned.1 = (bf16[128,512]{1,0:T(8,128)(2,1)S(1)}, bf16[128,512]{1,0:T(8,128)(2,1)S(1)}, f32[128,256]{1,0:T(8,128)S(1)}, f32[256,256]{1,0:T(8,128)S(1)}, bf16[25...) custom-call(s32[2,8]{1,0:T(2,128)S(1)} %compare_select_fusion.1.target_ref.refs_0_, f32[512,128]{1,0:T(8,128)S(1)} %copy-done.9, ...), custom_call_target="tpu_custom_call" | custom-call | tf_op jit(solution)/shard_map/turned/pallas_call | solution.py:151
  9.4 3.0 %collective-permute-done.1.cross_ref = bf16[512,256]{1,0:T(8,128)(2,1)} collective-permute-done((bf16[512,256]{1,0:T(8,128)(2,1)}, bf16[512,256]{1,0:T(8,128)(2,1)}, u32[]{:S(2)}, u32[]{:S(2)}) %collective-permute-start.1) | collective-permute-done | bytes 262176 | tf_op jit(solution)/shard_map/ppermute | solution.py:408
  12.3 3.0 %sweep.3 = (f32[512,256]{1,0:T(8,128)S(1)}, bf16[768,256]{1,0:T(8,128)(2,1)S(1)}, bf16[768,256]{1,0:T(8,128)(2,1)S(1)}) custom-call(s32[2,8]{1,0:T(2,128)S(1)} %compare_select_fusion.1.target_ref.refs_0_, bf16[512,256]{1,0:T(8,128)(2,1)} %get-tuple-element.26.own_ref, bf16[512,256]{1,0:T(8,128)(2,1)} %collective-permute-done.pair_ref, ...), custom_call_target="tpu_custom_call" | custom-call | tf_op jit(solution)/shard_map/sweep/pallas_call | solution.py:241
  15.4 3.6 %collective-permute-start.3 = (bf16[768,256]{1,0:T(8,128)(2,1)S(1)}, bf16[768,256]{1,0:T(8,128)(2,1)S(1)}, u32[]{:S(2)}, u32[]{:S(2)}) collective-permute-start(bf16[768,256]{1,0:T(8,128)(2,1)S(1)} %get-tuple-element.33), channel_id=1, source_target_pairs={{1,2},{2,1},{3,4},{4,3},{5,6},{6,5},{7,8},{8,7},{9,10},{10,9},{11,... | collective-permute-start | bytes 1179656 | tf_op jit(solution)/shard_map/ppermute | solution.py:408
  19.0 0.1 collective-permute-start.2
  19.1 0.3 projected.2.refs_0_.refs_1_
  19.4 0.8 copy-done
  20.2 4.3 %collective-permute-done.3.cross_ref = bf16[768,256]{1,0:T(8,128)(2,1)S(1)} collective-permute-done((bf16[768,256]{1,0:T(8,128)(2,1)S(1)}, bf16[768,256]{1,0:T(8,128)(2,1)S(1)}, u32[]{:S(2)}, u32[]{:S(2)}) %collective-permute-start.3) | collective-permute-done | bytes 393248 | tf_op jit(solution)/shard_map/ppermute | solution.py:408
  24.5 2.5 %sweep.4 = (f32[512,256]{1,0:T(8,128)S(1)}, bf16[512,256]{1,0:T(8,128)(2,1)S(1)}) custom-call(s32[2,8]{1,0:T(2,128)S(1)} %compare_select_fusion.1.target_ref.refs_0_, bf16[768,256]{1,0:T(8,128)(2,1)S(1)} %get-tuple-element.32.own_ref, bf16[768,256]{1,0:T(8,128)(2,1)S(1)} %collective-permute-done.2.pair_ref, ...), custom_call_target="tpu_custom_call" | custom-call | tf_op jit(solution)/shard_map/sweep/pallas_call | solution.py:241
  27.0 3.6 %collective-permute-start.5 = (bf16[512,256]{1,0:T(8,128)(2,1)S(1)}, bf16[512,256]{1,0:T(8,128)(2,1)S(1)}, u32[]{:S(2)}, u32[]{:S(2)}) collective-permute-start(bf16[512,256]{1,0:T(8,128)(2,1)S(1)} %get-tuple-element.35.own_ref), channel_id=1, source_target_pairs={{1,2},{2,1},{3,4},{4,3},{5,6},{6,5},{7,8},{8,7},{9,10},{10,9},{11,... | collective-permute-start | bytes 786440 | tf_op jit(solution)/shard_map/ppermute | solution.py:408
  30.6 0.1 collective-permute-start.4
  30.7 0.3 projected.3.refs_0_.refs_2_
  31.0 3.6 %collective-permute-done.5.cross_ref = bf16[512,256]{1,0:T(8,128)(2,1)S(1)} collective-permute-done((bf16[512,256]{1,0:T(8,128)(2,1)S(1)}, bf16[512,256]{1,0:T(8,128)(2,1)S(1)}, u32[]{:S(2)}, u32[]{:S(2)}) %collective-permute-start.5) | collective-permute-done | bytes 262176 | tf_op jit(solution)/shard_map/ppermute | solution.py:408
  34.7 2.5 %sweep.5 = (f32[512,256]{1,0:T(8,128)S(1)}, bf16[512,256]{1,0:T(8,128)(2,1)S(1)}) custom-call(s32[2,8]{1,0:T(2,128)S(1)} %compare_select_fusion.1.target_ref.refs_0_, bf16[512,256]{1,0:T(8,128)(2,1)S(1)} %get-tuple-element.35.own_ref, bf16[512,256]{1,0:T(8,128)(2,1)S(1)} %collective-permute-done.4.pair_ref, ...), custom_call_target="tpu_custom_call" | custom-call | tf_op jit(solution)/shard_map/sweep/pallas_call | solution.py:241
  37.2 0.4 packed.1
  37.5 0.8 copy-done.4
  38.4 0.8 copy-done.6
  39.1 0.7 copy-done.7
  39.8 19.3 %all-to-all-start = ((bf16[32,48,128]{2,1,0:T(8,128)(2,1)}), bf16[32,48,128]{2,1,0:T(8,128)(2,1)S(1)}, u32[]{:S(2)}, u32[]{:S(2)}) async-start(bf16[32,48,128]{2,1,0:T(8,128)(2,1)} %copy-done.6), calls=%async_computation | async-start | bytes 786432 | tf_op jit(solution)/shard_map/all_to_all | solution.py:384
  59.1 3.5 %collective-permute-start.7 = (bf16[512,256]{1,0:T(8,128)(2,1)}, bf16[512,256]{1,0:T(8,128)(2,1)}, u32[]{:S(2)}, u32[]{:S(2)}) collective-permute-start(bf16[512,256]{1,0:T(8,128)(2,1)} %copy-done.7), channel_id=1, source_target_pairs={{1,2},{2,1},{3,4},{4,3},{5,6},{6,5},{7,8},{8,7},{9,10},{10,9},{11,... | collective-permute-start | bytes 786440 | tf_op jit(solution)/shard_map/ppermute | solution.py:408
  62.7 0.1 collective-permute-start.6
  62.8 6.6 %all-to-all-done.in_ref = bf16[32,48,128]{2,1,0:T(8,128)(2,1)S(1)} async-done(((bf16[32,48,128]{2,1,0:T(8,128)(2,1)}), bf16[32,48,128]{2,1,0:T(8,128)(2,1)S(1)}, u32[]{:S(2)}, u32[]{:S(2)}) %all-to-all-start) | async-done | bytes 393248 | tf_op jit(solution)/shard_map/all_to_all | solution.py:384
  69.4 0.1 added.1.line_ref
  69.5 0.0 collective-permute-done.7.refs_3_
  69.5 1.1 copy-done.8
  70.6 3.0 %last_sweep.1 = (f32[512,256]{1,0:T(8,128)S(1)}, f32[8,40,128]{2,1,0:T(8,128)S(1)}) custom-call(f32[40,128]{1,0:T(8,128)S(1)} %added.1.line_ref, s32[2,8]{1,0:T(2,128)S(1)} %compare_select_fusion.1.target_ref.refs_0_, bf16[512,256]{1,0:T(8,128)(2,1)S(1)} %copy-done.8, bf16[512,256]{1,0:T(8,128)(2,1)} %collective-permute-done.6.refs_2_, ...), custom_call_target="tpu_custom_call" | custom-call | tf_op jit(solution)/shard_map/last_sweep/pallas_call | solution.py:207
  73.5 19.7 %all_to_all.15.in_ref = f32[8,40,128]{2,1,0:T(8,128)S(1)} all-to-all(f32[8,40,128]{2,1,0:T(8,128)S(1)} %get-tuple-element.40), channel_id=1, replica_groups=mesh['leaf_0'=8,'leaf_1'=4,'sib_0'=4,'sib_1'=2] {'leaf_0'}, dimensions={0} | all-to-all | bytes 327680 | tf_op jit(solution)/shard_map/all_to_all | solution.py:384
  93.2 17.3 %all_to_all.16.arrived_ref = bf16[32,48,128]{2,1,0:T(8,128)(2,1)S(1)} all-to-all(bf16[32,48,128]{2,1,0:T(8,128)(2,1)S(1)} %split.1), channel_id=1, replica_groups=mesh['leaf_0'=8,'leaf_1'=4,'sib_0'=4,'sib_1'=2] {'leaf_1','sib_0','sib_1'}, dimensions={0} | all-to-all | bytes 786432 | tf_op jit(solution)/shard_map/all_to_all | solution.py:384
  110.5 9.1 %last_step.1 = (f32[512,128]{1,0:T(8,128)}, f32[128,128]{1,0:T(8,128)}) custom-call(bf16[32,48,128]{2,1,0:T(8,128)(2,1)S(1)} %all_to_all.16.arrived_ref, f32[512,256]{1,0:T(8,128)S(1)} %get-tuple-element.22.basis_ref.refs_7_.refs_0_, f32[512,256]{1,0:T(8,128)S(1)} %copy-done.1, f32[512,256]{1,0:T(8,128)S(1)} %copy-done.3, f32[512,256]{1,0:T(8,128)S(1)} %copy-done.5, ...), custom_call_target="tpu_custom_call" | custom-call | tf_op jit(solution)/shard_map/last_step/pallas_call | solution.py:374
  (23 shorter events, 0.1 us)
Async XLA Ops:
  0.6 7.5 %copy-start.9 = (f32[512,128]{1,0:T(8,128)S(1)}, f32[512,128]{1,0:T(8,128)}, u32[]{:S(2)}) copy-start(f32[512,128]{1,0:T(8,128)} %factor_ref.1) | copy-start | bytes 786436
  0.6 7.5 %copy-start.10 = (s32[2,8]{1,0:T(2,128)S(1)}, s32[2,8]{1,0:T(2,128)}, u32[]{:S(2)}) copy-start(s32[2,8]{1,0:T(2,128)} %param.11) | copy-start | bytes 196
  3.4 8.9 %collective-permute-start.1 = (bf16[512,256]{1,0:T(8,128)(2,1)}, bf16[512,256]{1,0:T(8,128)(2,1)}, u32[]{:S(2)}, u32[]{:S(2)}) collective-permute-start(bf16[512,256]{1,0:T(8,128)(2,1)} %get-tuple-element.26.own_ref), channel_id=1, source_target_pairs={{1,2},{2,1},{3,4},{4,3},{5,6},{6,5},{7,8},{8,7},{9,10},{10,9},{11,... | collective-permute-start | bytes 786440 | tf_op jit(solution)/shard_map/ppermute | solution.py:408
  8.0 4.4 %collective-permute-start = (bf16[512,256]{1,0:T(8,128)(2,1)}, bf16[512,256]{1,0:T(8,128)(2,1)}, u32[]{:S(2)}, u32[]{:S(2)}) collective-permute-start(bf16[512,256]{1,0:T(8,128)(2,1)} %get-tuple-element.26.own_ref), channel_id=1, source_target_pairs={{0,1},{1,0},{2,3},{3,2},{4,5},{5,4},{6,7},{7,6},{8,9},{9,8},{10,11... | collective-permute-start | bytes 786440 | tf_op jit(solution)/shard_map/ppermute | solution.py:409
  15.4 9.1 %collective-permute-start.3 = (bf16[768,256]{1,0:T(8,128)(2,1)S(1)}, bf16[768,256]{1,0:T(8,128)(2,1)S(1)}, u32[]{:S(2)}, u32[]{:S(2)}) collective-permute-start(bf16[768,256]{1,0:T(8,128)(2,1)S(1)} %get-tuple-element.33), channel_id=1, source_target_pairs={{1,2},{2,1},{3,4},{4,3},{5,6},{6,5},{7,8},{8,7},{9,10},{10,9},{11,... | collective-permute-start | bytes 1179656 | tf_op jit(solution)/shard_map/ppermute | solution.py:408
  19.0 5.4 %collective-permute-start.2 = (bf16[768,256]{1,0:T(8,128)(2,1)S(1)}, bf16[768,256]{1,0:T(8,128)(2,1)S(1)}, u32[]{:S(2)}, u32[]{:S(2)}) collective-permute-start(bf16[768,256]{1,0:T(8,128)(2,1)S(1)} %get-tuple-element.32.own_ref), channel_id=1, source_target_pairs={{0,1},{1,0},{2,3},{3,2},{4,5},{5,4},{6,7},{7,6},{8,9},{9,8},{10,11... | collective-permute-start | bytes 1179656 | tf_op jit(solution)/shard_map/ppermute | solution.py:409
  19.4 0.8 copy-start
  27.0 10.2 %copy-start.2 = (f32[512,256]{1,0:T(8,128)}, f32[512,256]{1,0:T(8,128)S(1)}, u32[]{:S(2)}) copy-start(f32[512,256]{1,0:T(8,128)S(1)} %get-tuple-element.36.value_ref.refs_2_) | copy-start | bytes 1572868
  27.0 7.7 %collective-permute-start.5 = (bf16[512,256]{1,0:T(8,128)(2,1)S(1)}, bf16[512,256]{1,0:T(8,128)(2,1)S(1)}, u32[]{:S(2)}, u32[]{:S(2)}) collective-permute-start(bf16[512,256]{1,0:T(8,128)(2,1)S(1)} %get-tuple-element.35.own_ref), channel_id=1, source_target_pairs={{1,2},{2,1},{3,4},{4,3},{5,6},{6,5},{7,8},{8,7},{9,10},{10,9},{11,... | collective-permute-start | bytes 786440 | tf_op jit(solution)/shard_map/ppermute | solution.py:408
  30.6 4.0 %collective-permute-start.4 = (bf16[512,256]{1,0:T(8,128)(2,1)S(1)}, bf16[512,256]{1,0:T(8,128)(2,1)S(1)}, u32[]{:S(2)}, u32[]{:S(2)}) collective-permute-start(bf16[512,256]{1,0:T(8,128)(2,1)S(1)} %get-tuple-element.35.own_ref), channel_id=1, source_target_pairs={{0,1},{1,0},{2,3},{3,2},{4,5},{5,4},{6,7},{7,6},{8,9},{9,8},{10,11... | collective-permute-start | bytes 786440 | tf_op jit(solution)/shard_map/ppermute | solution.py:409
  37.5 0.8 copy-start.4
  38.3 0.8 copy-start.6
  39.1 0.7 copy-start.7
  39.8 29.6 %all-to-all-start = ((bf16[32,48,128]{2,1,0:T(8,128)(2,1)}), bf16[32,48,128]{2,1,0:T(8,128)(2,1)S(1)}, u32[]{:S(2)}, u32[]{:S(2)}) async-start(bf16[32,48,128]{2,1,0:T(8,128)(2,1)} %copy-done.6), calls=%async_computation | async-start | bytes 786432 | tf_op jit(solution)/shard_map/all_to_all | solution.py:384
  59.1 10.4 %collective-permute-start.7 = (bf16[512,256]{1,0:T(8,128)(2,1)}, bf16[512,256]{1,0:T(8,128)(2,1)}, u32[]{:S(2)}, u32[]{:S(2)}) collective-permute-start(bf16[512,256]{1,0:T(8,128)(2,1)} %copy-done.7), channel_id=1, source_target_pairs={{1,2},{2,1},{3,4},{4,3},{5,6},{6,5},{7,8},{8,7},{9,10},{10,9},{11,... | collective-permute-start | bytes 786440 | tf_op jit(solution)/shard_map/ppermute | solution.py:408
  62.7 6.8 %collective-permute-start.6 = (bf16[512,256]{1,0:T(8,128)(2,1)}, bf16[512,256]{1,0:T(8,128)(2,1)}, u32[]{:S(2)}, u32[]{:S(2)}) collective-permute-start(bf16[512,256]{1,0:T(8,128)(2,1)} %copy-done.7), channel_id=1, source_target_pairs={{0,1},{1,0},{2,3},{3,2},{4,5},{5,4},{6,7},{7,6},{8,9},{9,8},{10,11... | collective-permute-start | bytes 786440 | tf_op jit(solution)/shard_map/ppermute | solution.py:409
  69.5 41.0 %copy-start.1 = (f32[512,256]{1,0:T(8,128)S(1)}, f32[512,256]{1,0:T(8,128)}, u32[]{:S(2)}) copy-start(f32[512,256]{1,0:T(8,128)} %copy-done) | copy-start | bytes 1572868
  69.5 41.0 %copy-start.3 = (f32[512,256]{1,0:T(8,128)S(1)}, f32[512,256]{1,0:T(8,128)}, u32[]{:S(2)}) copy-start(f32[512,256]{1,0:T(8,128)} %copy-done.2) | copy-start | bytes 1572868
  69.5 41.0 %copy-start.5 = (f32[512,256]{1,0:T(8,128)S(1)}, f32[512,256]{1,0:T(8,128)}, u32[]{:S(2)}) copy-start(f32[512,256]{1,0:T(8,128)} %copy-done.4) | copy-start | bytes 1572868
  69.5 1.1 copy-start.8
